TPU v7x, 256 devices: a whole 4x4x8 slice. The times are simulated.
256 devices in a mesh: cell: 64 (over x, z_hi, y, core), cls: 4 (over z_lo).
Axes of the slice: x: 4, y: 4, z: 8 (z_hi: 2, z_lo: 4; z = z_hi * 4 + z_lo), core: 2. Of those that a mesh axis runs over, the one named last changes fastest.
Arguments:
- melt: float32 [64, 32, 65536], P(None, 'cls', 'cell'), may hold values from 0 to 1
- counts: int32 [32, 65536], P('cls', 'cell'), may hold values from 0 to 800, as said below
- pressure: float32 [256, 256], P(('cell', 'cls')), may hold values from 0.5 to 2
- propagator: float32 [32, 64, 64], replicated, as said below
- coupling: float32 [32, 64], replicated, may hold values from 0.05 to 0.5
- flux_weights: float32 [32, 64], replicated, may hold values from 0.002 to 0.2
Outputs:
- shells_out: float32 [64, 32, 65536], P(None, 'cls', 'cell')
- pressure_out: float32 [256, 256], P(('cell', 'cls'))
Inputs may be any that keep to these rules, and one draw needn't show every extreme that they name: counts in layer l are non-negative and below 201 + (600 * l) // 255. Each propagator matrix has a dominant diagonal.
All inputs are finite; a program needn't handle non-finite values.
Results may differ from a plain program's by a relative error of at most 0.0001.
Values sent between devices are 32-bit elements; how exact they have to be, the bound alone decides.
A program may use at most 64 MiB of HBM per device.

v0:
```python
import jax
import jax.numpy as jnp
from jax import lax
from jax.sharding import PartitionSpec as P

CLASSES = 32
SIDE = 16
SUBSTEPS = 4


count_scale = 400.0


def extended_2(block, sides, width):
    for axis, dim in sides:
        count = lax.axis_size(axis)
        forward = [(i, i + 1) for i in range(count - 1)]
        backward = [(target, source) for source, target in forward]
        low = lax.ppermute(
            lax.slice_in_dim(block, block.shape[dim] - width, None, axis=dim), axis, forward
        )
        high = lax.ppermute(lax.slice_in_dim(block, 0, width, axis=dim), axis, backward)
        block = jnp.concatenate([low, block, high], axis=dim)
    return block


def shell_update(shells, counts_f, propagator, coupling, flux_weights, wall):
    shells = (
        jnp.einsum("kij,jkc->ikc", propagator, shells, precision=lax.Precision.HIGHEST)
        + coupling.T[:, :, None] * wall[None, None, :]
    )
    flux = jnp.einsum("ki,ikc->kc", flux_weights, shells, precision=lax.Precision.HIGHEST)
    partial_gas = jnp.sum(counts_f * flux, axis=0) / (count_scale * CLASSES)
    return (shells, partial_gas)


def pressure_update(tile, gas_tile):
    total = lax.psum(jnp.sum(gas_tile), ("cell", "cls"))
    all_cells = gas_tile.shape[0] * lax.axis_size("cell") * lax.axis_size("cls")
    chamber = 1.5 - 0.5 * total / all_cells
    layer_count = tile.shape[0]
    field = tile.reshape(layer_count, SIDE, SIDE)
    extended = extended_2(field, ((("cell", "cls"), 0),), 1)
    extended = jnp.pad(extended, ((0, 0), (1, 1), (1, 1)))
    lap = (
        extended[2:, 1:-1, 1:-1]
        + extended[:-2, 1:-1, 1:-1]
        + extended[1:-1, 2:, 1:-1]
        + extended[1:-1, :-2, 1:-1]
        + extended[1:-1, 1:-1, 2:]
        + extended[1:-1, 1:-1, :-2]
        - 6.0 * field
    )
    field = field + 0.15 * lap + 0.1 * gas_tile.reshape(field.shape) + 0.2 * (chamber - field)
    return field.reshape(tile.shape)


def shards(melt, counts, pressure, propagator, coupling, flux_weights):
    tile = pressure
    class_count = melt.shape[1]
    start = lax.axis_index("cls") * class_count
    local_prop = lax.dynamic_slice_in_dim(propagator, start, class_count, 0)
    local_coupling = lax.dynamic_slice_in_dim(coupling, start, class_count, 0)
    local_flux = lax.dynamic_slice_in_dim(flux_weights, start, class_count, 0)
    counts_f = counts.astype(jnp.float32)
    shells = melt
    for step in range(SUBSTEPS):
        block_pressure = lax.all_gather(tile.reshape(-1), "cls", axis=0, tiled=True)
        shells, partial_gas = shell_update(
            shells, counts_f, local_prop, local_coupling, local_flux, 0.5 * block_pressure
        )
        gas_tile = lax.psum_scatter(partial_gas, "cls", scatter_dimension=0, tiled=True)
        tile = pressure_update(tile, gas_tile)
    return (shells, tile)


def solution(mesh):
    placed = (P(None, "cls", "cell"), P("cls", "cell"), P(("cell", "cls"), None), P(), P(), P())
    return jax.shard_map(
        shards,
        mesh=mesh,
        in_specs=placed,
        out_specs=(P(None, "cls", "cell"), P(("cell", "cls"), None)),
        check_vma=False,
    )
```

profile of v0, /device:TPU:1, one launch (start us, length us, event | category | flops | bytes accessed | tf_op | source)
XLA Modules:
  0.0 445.1 jit_solution(3294544564548670002)
XLA Ops:
  0.6 0.5 broadcast.251
  1.2 1.5 reduce.3
  2.7 4.4 collective-permute-start.1
  7.1 5.2 %collective-permute-start = (f32[1,16,16]{2,1,0:T(8,128)S(1)}, f32[1,16,16]{2,1,0:T(8,128)S(1)}, u32[]{:S(2)}, u32[]{:S(2)}) collective-permute-start(f32[1,16,16]{2,1,0:T(8,128)S(1)} %reshape.107), channel_id=1, source_target_pairs={{1,0},{2,1},{3,2},{4,3},{5,4},{6,5},{7,6},{8,7},{9,8},{10,9},{11,1... | collective-permute-start | bytes 3080 | tf_op jit(solution)/shard_map/ppermute | solution.py:22
  12.3 7.0 %all-gather = f32[1,1024]{1,0:T(1,128)S(1)} all-gather(f32[1,256]{1,0:T(1,128)} %param.8), channel_id=2, replica_groups=mesh['cell'=64,'cls'=4] {'cls'}, dimensions={1}, use_global_device_ids=true | all-gather | bytes 5120 | tf_op jit(solution)/shard_map/all_gather | solution.py:68
  19.2 1.3 dynamic-slice
  21.2 0.7 dynamic-slice_bitcast_fusion
  21.9 4.0 fusion
  25.9 1.3 copy-done.1
  27.2 1.3 fusion.2
  28.6 7.5 %all-reduce.4 = f32[1024]{0:T(1024)S(1)} all-reduce(f32[1024]{0:T(1024)S(1)} %broadcast_multiply_fusion.7), channel_id=3, replica_groups=mesh['cell'=64,'cls'=4] {'cls'}, use_global_device_ids=true, to_apply=%region_1.0.clone | all-reduce | flops 1024 | bytes 8192
  36.1 0.7 dynamic-slice_reduce_fusion.3
  36.7 80.6 %psum.28 = f32[]{:T(128)} all-reduce(f32[]{:T(128)} %get-tuple-element.12), channel_id=1, replica_groups=mesh['cell'=64,'cls'=4] {'cell','cls'}, use_global_device_ids=true, to_apply=%region_3.0 | all-reduce | flops 1 | bytes 8 | tf_op jit(solution)/shard_map/psum | solution.py:38
  118.1 0.1 select_maximum_fusion.6
  118.2 0.1 fusion.45
  118.3 3.5 collective-permute-start.3
  121.8 4.4 collective-permute-start.2
  126.2 6.7 %all-gather.1 = f32[4,1,256]{2,1,0:T(1,128)S(1)} all-gather(f32[1,1,256]{2,1,0:T(1,128)S(1)} %reshape.112), channel_id=1, replica_groups=mesh['cell'=64,'cls'=4] {'cls'}, dimensions={0}, use_global_device_ids=true | all-gather | bytes 5120 | tf_op jit(solution)/shard_map/all_gather | solution.py:68
  132.9 3.9 bitcast_add_fusion.2
  136.9 1.1 fusion.50
  138.0 3.3 fusion.15
  141.3 7.5 %all-reduce.5 = f32[1024]{0:T(1024)S(1)} all-reduce(f32[1024]{0:T(1024)S(1)} %broadcast_multiply_fusion.6), channel_id=4, replica_groups=mesh['cell'=64,'cls'=4] {'cls'}, use_global_device_ids=true, to_apply=%region_5.6.clone | all-reduce | flops 1024 | bytes 8192
  148.8 0.7 dynamic-slice_reduce_fusion.2
  149.5 78.4 %psum.29 = f32[]{:T(128)} all-reduce(f32[]{:T(128)} %get-tuple-element.10), channel_id=1, replica_groups=mesh['cell'=64,'cls'=4] {'cell','cls'}, use_global_device_ids=true, to_apply=%region_7.8 | all-reduce | flops 1 | bytes 8 | tf_op jit(solution)/shard_map/psum | solution.py:38
  228.6 0.1 select_maximum_fusion.4
  228.7 0.1 fusion.40
  228.9 3.7 collective-permute-start.5
  232.6 3.8 collective-permute-start.4
  236.4 6.5 %all-gather.2 = f32[4,1,256]{2,1,0:T(1,128)S(1)} all-gather(f32[1,1,256]{2,1,0:T(1,128)S(1)} %reshape.114), channel_id=1, replica_groups=mesh['cell'=64,'cls'=4] {'cls'}, dimensions={0}, use_global_device_ids=true | all-gather | bytes 5120 | tf_op jit(solution)/shard_map/all_gather | solution.py:68
  242.8 2.9 fusion.4
  245.8 7.8 %all-reduce.6 = f32[1024]{0:T(1024)S(1)} all-reduce(f32[1024]{0:T(1024)S(1)} %broadcast_multiply_fusion.5), channel_id=5, replica_groups=mesh['cell'=64,'cls'=4] {'cls'}, use_global_device_ids=true, to_apply=%region_9.10.clone | all-reduce | flops 1024 | bytes 8192
  253.5 0.7 dynamic-slice_reduce_fusion.1
  254.2 77.2 %psum.30 = f32[]{:T(128)} all-reduce(f32[]{:T(128)} %get-tuple-element.8), channel_id=1, replica_groups=mesh['cell'=64,'cls'=4] {'cell','cls'}, use_global_device_ids=true, to_apply=%region_11.12 | all-reduce | flops 1 | bytes 8 | tf_op jit(solution)/shard_map/psum | solution.py:38
  332.2 0.1 select_maximum_fusion.2
  332.3 0.1 fusion.35
  332.4 3.7 collective-permute-start.7
  336.1 3.7 collective-permute-start.6
  339.8 6.1 %all-gather.3 = f32[4,1,256]{2,1,0:T(1,128)S(1)} all-gather(f32[1,1,256]{2,1,0:T(1,128)S(1)} %reshape.116), channel_id=1, replica_groups=mesh['cell'=64,'cls'=4] {'cls'}, dimensions={0}, use_global_device_ids=true | all-gather | bytes 5120 | tf_op jit(solution)/shard_map/all_gather | solution.py:68
  345.9 3.9 bitcast_add_fusion
  349.9 1.3 copy-done.2
  351.2 1.1 fusion.51
  352.3 8.0 %all-reduce.7 = f32[1024]{0:T(1024)S(1)} all-reduce(f32[1024]{0:T(1024)S(1)} %broadcast_multiply_fusion.4), channel_id=6, replica_groups=mesh['cell'=64,'cls'=4] {'cls'}, use_global_device_ids=true, to_apply=%region_13.14.clone | all-reduce | flops 1024 | bytes 8192
  360.3 0.7 dynamic-slice_reduce_fusion
  361.0 78.4 %psum.31 = f32[]{:T(128)} all-reduce(f32[]{:T(128)} %get-tuple-element.6), channel_id=1, replica_groups=mesh['cell'=64,'cls'=4] {'cell','cls'}, use_global_device_ids=true, to_apply=%region_15.16 | all-reduce | flops 1 | bytes 8 | tf_op jit(solution)/shard_map/psum | solution.py:38
  439.4 4.1 copy.11
  444.3 0.1 select_maximum_fusion
  444.4 0.1 fusion.30
  444.4 0.6 reshape.108
  (36 shorter events, 0.8 us)
Async XLA Ops:
  0.6 21.2 %copy-start = (f32[64,8,1024]{2,1,0:T(8,128)S(1)}, f32[64,8,1024]{2,1,0:T(8,128)}, u32[]{:S(2)}) copy-start(f32[64,8,1024]{2,1,0:T(8,128)} %param.6) | copy-start | bytes 6291460
  2.7 115.4 %collective-permute-start.1 = (f32[1,16,16]{2,1,0:T(8,128)S(1)}, f32[1,16,16]{2,1,0:T(8,128)S(1)}, u32[]{:S(2)}, u32[]{:S(2)}) collective-permute-start(f32[1,16,16]{2,1,0:T(8,128)S(1)} %reshape.107), channel_id=1, source_target_pairs={{0,1},{1,2},{2,3},{3,4},{4,5},{5,6},{6,7},{7,8},{8,9},{9,10},{10,1... | collective-permute-start | bytes 3080 | tf_op jit(solution)/shard_map/ppermute | solution.py:19
  7.1 111.0 %collective-permute-start = (f32[1,16,16]{2,1,0:T(8,128)S(1)}, f32[1,16,16]{2,1,0:T(8,128)S(1)}, u32[]{:S(2)}, u32[]{:S(2)}) collective-permute-start(f32[1,16,16]{2,1,0:T(8,128)S(1)} %reshape.107), channel_id=1, source_target_pairs={{1,0},{2,1},{3,2},{4,3},{5,4},{6,5},{7,6},{8,7},{9,8},{10,9},{11,1... | collective-permute-start | bytes 3080 | tf_op jit(solution)/shard_map/ppermute | solution.py:22
  25.9 1.3 copy-start.1
  25.9 2.6 copy-start.4
  25.9 107.0 %copy-start.3 = (f32[32,64,64]{2,1,0:T(8,128)S(1)}, f32[32,64,64]{2,1,0:T(8,128)}, u32[]{:S(2)}) copy-start(f32[32,64,64]{2,1,0:T(8,128)} %param.9) | copy-start | bytes 1572868
  118.3 110.3 %collective-permute-start.3 = (f32[1,16,16]{2,1,0:T(8,128)S(1)}, f32[1,16,16]{2,1,0:T(8,128)S(1)}, u32[]{:S(2)}, u32[]{:S(2)}) collective-permute-start(f32[1,16,16]{2,1,0:T(8,128)S(1)} %fusion.45), channel_id=1, source_target_pairs={{0,1},{1,2},{2,3},{3,4},{4,5},{5,6},{6,7},{7,8},{8,9},{9,10},{10,1... | collective-permute-start | bytes 3080 | tf_op jit(solution)/shard_map/ppermute | solution.py:19
  121.8 106.8 %collective-permute-start.2 = (f32[1,16,16]{2,1,0:T(8,128)S(1)}, f32[1,16,16]{2,1,0:T(8,128)S(1)}, u32[]{:S(2)}, u32[]{:S(2)}) collective-permute-start(f32[1,16,16]{2,1,0:T(8,128)S(1)} %fusion.45), channel_id=1, source_target_pairs={{1,0},{2,1},{3,2},{4,3},{5,4},{6,5},{7,6},{8,7},{9,8},{10,9},{11,1... | collective-permute-start | bytes 3080 | tf_op jit(solution)/shard_map/ppermute | solution.py:22
  228.9 103.3 %collective-permute-start.5 = (f32[1,16,16]{2,1,0:T(8,128)S(1)}, f32[1,16,16]{2,1,0:T(8,128)S(1)}, u32[]{:S(2)}, u32[]{:S(2)}) collective-permute-start(f32[1,16,16]{2,1,0:T(8,128)S(1)} %fusion.40), channel_id=1, source_target_pairs={{0,1},{1,2},{2,3},{3,4},{4,5},{5,6},{6,7},{7,8},{8,9},{9,10},{10,1... | collective-permute-start | bytes 3080 | tf_op jit(solution)/shard_map/ppermute | solution.py:19
  232.6 99.6 %collective-permute-start.4 = (f32[1,16,16]{2,1,0:T(8,128)S(1)}, f32[1,16,16]{2,1,0:T(8,128)S(1)}, u32[]{:S(2)}, u32[]{:S(2)}) collective-permute-start(f32[1,16,16]{2,1,0:T(8,128)S(1)} %fusion.40), channel_id=1, source_target_pairs={{1,0},{2,1},{3,2},{4,3},{5,4},{6,5},{7,6},{8,7},{9,8},{10,9},{11,1... | collective-permute-start | bytes 3080 | tf_op jit(solution)/shard_map/ppermute | solution.py:22
  332.4 111.8 %collective-permute-start.7 = (f32[1,16,16]{2,1,0:T(8,128)S(1)}, f32[1,16,16]{2,1,0:T(8,128)S(1)}, u32[]{:S(2)}, u32[]{:S(2)}) collective-permute-start(f32[1,16,16]{2,1,0:T(8,128)S(1)} %fusion.35), channel_id=1, source_target_pairs={{0,1},{1,2},{2,3},{3,4},{4,5},{5,6},{6,7},{7,8},{8,9},{9,10},{10,1... | collective-permute-start | bytes 3080 | tf_op jit(solution)/shard_map/ppermute | solution.py:19
  336.1 108.2 %collective-permute-start.6 = (f32[1,16,16]{2,1,0:T(8,128)S(1)}, f32[1,16,16]{2,1,0:T(8,128)S(1)}, u32[]{:S(2)}, u32[]{:S(2)}) collective-permute-start(f32[1,16,16]{2,1,0:T(8,128)S(1)} %fusion.35), channel_id=1, source_target_pairs={{1,0},{2,1},{3,2},{4,3},{5,4},{6,5},{7,6},{8,7},{9,8},{10,9},{11,1... | collective-permute-start | bytes 3080 | tf_op jit(solution)/shard_map/ppermute | solution.py:22
  349.9 1.4 copy-start.2
where the time goes:
time: 446 us; the launch traced here: 445 us
  blocking collectives  372 us (83%)
  starting transfers between devices  32.2 us (7%)
  matrix products  21.6 us (5%)
  local copies, waits for them, and re-layouts  10.6 us (2%)
  other arithmetic  4.92 us (1%)
    psum x4, blocking collectives, pressure_update(): total = lax.psum(jnp.sum(gas_tile), ('cell', 'cls'))  315 us
    unnamed x4, blocking collectives  30.7 us
    all_gather x4, blocking collectives, shards(): block_pressure = lax.all_gather(tile.reshape(-1), 'cls', axis=0, tiled=True)  26.3 us
    ppermute x4, starting transfers between devices, extended_2(): lax.ppermute(lax.slice_in_dim(block, 0, width, axis=dim), axis, backward)  17 us
    ppermute x4, starting transfers between devices, extended_2(): lax.ppermute(lax.slice_in_dim(block, block.shape[dim] - width, None, axis...  15.2 us
    dot_general x4, matrix products, shell_update(): jnp.einsum('kij,jkc->ikc', propagator, shells, precision=lax.Precision.HI...  15.2 us
  transfers between devices with their start and end apart: 8, of which 0 were waited for; matrix products, arithmetic and copies ran while one was open for 7% of the time, Pallas kernels for 0%

commit v1 on v0

v1 whole, which is shorter than its diff:
```python
import functools

import jax
import jax.numpy as jnp
from jax import lax
from jax.experimental import pallas as pl
from jax.experimental.pallas import tpu as pltpu
from jax.sharding import PartitionSpec as P

MESH = pl.DeviceIdType.MESH
F32 = jnp.float32
BF16 = jnp.bfloat16
NODES = 64
CLASSES = 32
SIDE = 16
PLANE = 256
LAYERS = 4
BLOCK = LAYERS * PLANE
KC = 8
NCELLS = 65536
COUNT_SCALE = 400.0
CHUNKS = 8


def split2(x):
    hi = x.astype(BF16)
    return hi, (x - hi.astype(F32)).astype(BF16)


def dot_nn(a, b):
    return jnp.dot(a, b, preferred_element_type=F32)


def dot3(a, b):
    (ah, al), (bh, bl) = a, b
    return dot_nn(ah, bh) + (dot_nn(al, bh) + dot_nn(ah, bl))


def main_kernel(
    melt_hbm, counts_hbm, pres_ref, prop_hbm, coup_hbm, fw_hbm,
    m_ref, walls_ref, vec_ref, pout_ref,
    melt_v, counts_ref, prop_v, coup_v, fw_v, part, p0, acc_a, acc_b, srow, pbuf,
    load_sem, small_sem, part_send, part_recv, p_send, p_recv, a_send, a_recv, b_send, b_recv,
):
    cell = lax.axis_index("cell")
    cls = lax.axis_index("cls")
    core = cell % 2
    yy = (cell // 2) % 4
    zh = (cell // 8) % 2
    xx = cell // 16
    has_prev = cell > 0
    has_next = cell < 63

    loads = [
        pltpu.make_async_copy(melt_hbm.at[:, pl.ds(i * 128, 128)], melt_v.at[i], load_sem.at[i])
        for i in range(CHUNKS)
    ]
    smalls = [
        pltpu.make_async_copy(prop_hbm.at[pl.ds(cls * 512, 512)], prop_v, small_sem.at[0]),
        pltpu.make_async_copy(coup_hbm.at[pl.ds(cls * 8, 8)], coup_v, small_sem.at[1]),
        pltpu.make_async_copy(fw_hbm.at[pl.ds(cls * 8, 8)], fw_v, small_sem.at[2]),
        pltpu.make_async_copy(counts_hbm, counts_ref, small_sem.at[3]),
        pltpu.make_async_copy(pres_ref, p0.at[1, cls], small_sem.at[4]),
    ]
    for copy in smalls + loads:
        copy.start()

    barrier = pltpu.get_barrier_semaphore()

    def signal(c, k):
        pl.semaphore_signal(barrier, inc=1, device_id=(c, k), device_id_type=MESH)

    def stage_a_peer(d):
        s = (yy * 2 + core + d) % 8
        return (cell // 8) * 8 + s

    def block_at(x, z, y, c):
        return ((x * 2 + z) * 4 + y) * 2 + c

    is_edge = jnp.logical_or(cls == 0, cls == 3)
    near = jnp.where(cls == 3, 0, 3)
    near2 = jnp.where(cls == 3, 1, 2)
    source = jnp.where(cls < 2, 3, 0)

    for d in range(1, 4):
        signal(cell, (cls + d) % 4)
    for d in range(1, 8):
        signal(stage_a_peer(d), cls)
    for d in range(1, 4):
        signal(block_at((xx + d) % 4, zh, yy, core), cls)
    for d in range(4):
        signal(block_at((xx + d) % 4, 1 - zh, yy, core), source)

    @pl.when(has_prev)
    def _():
        for k in range(4):
            signal(cell - 1, k)

    @pl.when(has_next)
    def _():
        for k in range(4):
            signal(cell + 1, k)

    one = jnp.int32(1)
    greeted = 13 + 8 * jnp.where(is_edge, one, 0) + 4 * jnp.where(has_prev, one, 0) + 4 * jnp.where(has_next, one, 0)
    pl.semaphore_wait(barrier, greeted)

    def p_copy(rel, d, c, k):
        return pltpu.make_async_remote_copy(
            src_ref=pres_ref, dst_ref=p0.at[rel, cls], send_sem=p_send.at[rel, d],
            recv_sem=p_recv.at[rel, cls], device_id=(c, k), device_id_type=MESH)

    def part_copy(rel, d, c, k):
        lo = {0: PLANE, 1: 0, 2: 0}[rel]
        n = {0: 3 * PLANE, 1: BLOCK, 2: 3 * PLANE}[rel]
        return pltpu.make_async_remote_copy(
            src_ref=part.at[1, cls, :, pl.ds(lo, n)], dst_ref=part.at[rel, cls, :, pl.ds(lo, n)],
            send_sem=part_send.at[rel, d], recv_sem=part_recv.at[rel, cls],
            device_id=(c, k), device_id_type=MESH)

    def send_all(make):
        for d in range(1, 4):
            make(1, d, cell, (cls + d) % 4).start()

        @pl.when(has_prev)
        def _():
            for k in range(4):
                make(2, k, cell - 1, k).start()

        @pl.when(has_next)
        def _():
            for k in range(4):
                make(0, k, cell + 1, k).start()

    def wait_sends(make):
        for d in range(1, 4):
            make(1, d, cell, (cls + d) % 4).wait_send()

        @pl.when(has_prev)
        def _():
            for k in range(4):
                make(2, k, cell - 1, k).wait_send()

        @pl.when(has_next)
        def _():
            for k in range(4):
                make(0, k, cell + 1, k).wait_send()

    def p_arrival(rel, k):
        return pltpu.make_async_copy(p0.at[rel, k], p0.at[rel, k], p_recv.at[rel, k])

    def part_arrival(rel, k):
        lo = {0: PLANE, 1: 0, 2: 0}[rel]
        n = {0: 3 * PLANE, 1: BLOCK, 2: 3 * PLANE}[rel]
        ref = part.at[rel, k, :, pl.ds(lo, n)]
        return pltpu.make_async_copy(ref, ref, part_recv.at[rel, k])

    def wait_arrivals(arrival):
        for d in range(1, 4):
            arrival(1, (cls + d) % 4).wait()

        @pl.when(has_prev)
        def _():
            for k in range(4):
                arrival(0, k).wait()

        @pl.when(has_next)
        def _():
            for k in range(4):
                arrival(2, k).wait()

    send_all(p_copy)

    @pl.when(jnp.logical_not(has_prev))
    def _():
        p0[0] = jnp.zeros((4, 1, PLANE), F32)
        part[0] = jnp.zeros((4, KC, BLOCK), F32)

    @pl.when(jnp.logical_not(has_next))
    def _():
        p0[2] = jnp.zeros((4, 1, PLANE), F32)
        part[2] = jnp.zeros((4, KC, BLOCK), F32)

    for copy in smalls:
        copy.wait()
    prop = prop_v[...]
    p_hi, p_lo = split2(prop)
    pp = jnp.concatenate([p_hi, p_lo], axis=1)
    lane = lax.broadcasted_iota(jnp.int32, (KC, 128), 1)
    row = lax.broadcasted_iota(jnp.int32, (KC, 128), 0)
    half = jnp.where(lane >= 64, 1, 0)

    def doubled(x):
        return jnp.concatenate([x, x], axis=1)

    def kron(x):
        return jnp.concatenate([jnp.where(row == 2 * v + half, x, 0.0) for v in range(4)], axis=1)

    def row_step(r):
        hi, lo = split2(kron(r))
        y = dot_nn(jnp.concatenate([hi, lo], axis=0), pp)
        y = y[:KC] + y[KC:]
        return y + pltpu.roll(y, 64, 1)

    fw = fw_v[...]
    coup = coup_v[...]
    rs = [doubled(fw)]
    for t in range(4):
        rs.append(row_step(rs[-1]))

    counts_f = counts_ref[...].astype(F32)
    for i, copy in enumerate(loads):
        copy.wait()
    acc = [[jnp.zeros((KC, 128), F32) for _ in range(CHUNKS)] for _ in range(4)]
    for j in range(NODES):
        factors = [jnp.broadcast_to(rs[t + 1][:, j : j + 1], (KC, 128)) for t in range(4)]
        for i in range(CHUNKS):
            node = melt_v[i, pl.ds(j * KC, KC), :]
            for t in range(4):
                acc[t][i] = acc[t][i] + factors[t] * node
    scale = 1.0 / (COUNT_SCALE * CLASSES)
    for t in range(4):
        flux = jnp.concatenate(acc[t], axis=1)
        part[1, cls, t : t + 1, :] = jnp.sum(counts_f * flux, axis=0, keepdims=True) * scale
        a_t = jnp.sum(rs[t][:, :NODES] * coup, axis=1, keepdims=True)
        part[1, cls, 4 + t : 5 + t, :] = jnp.sum(counts_f * a_t, axis=0, keepdims=True) * scale

    send_all(part_copy)

    def col_step(v):
        hi, lo = split2(v[:, :NODES])
        lhs = jnp.concatenate([hi, lo], axis=0)
        nt = (((1,), (1,)), ((), ()))
        y = lax.dot_general(lhs, p_hi, nt, preferred_element_type=F32)
        y = y[:KC] + y[KC:] + lax.dot_general(hi, p_lo, nt, preferred_element_type=F32)
        z = jnp.zeros((KC, 128), F32)
        for q in range(4):
            z = z + jnp.where(row == 2 * q + half, y[:, 128 * q : 128 * (q + 1)], 0.0)
        return z + pltpu.roll(z, 64, 1)

    vs = [doubled(coup)]
    for s in range(3):
        vs.append(col_step(vs[-1]))
    for s in range(4):
        for j in range(NODES):
            vec_ref[s, pl.ds(j * KC, KC), :] = jnp.broadcast_to(vs[3 - s][:, j : j + 1], (KC, 128))

    for k in range(KC):
        one = split2(prop[k * NODES : (k + 1) * NODES, :])
        two = split2(dot3(one, one))
        four_hi, four_lo = split2(dot3(two, two))
        lhs = jnp.concatenate([four_hi, four_lo], axis=0)

        def columns(n, carry, lhs=lhs, four_hi=four_hi, k=k):
            at = pl.ds(k, NODES, stride=KC)
            x_hi, x_lo = split2(melt_v[n, at, :])
            y = dot_nn(lhs, x_hi)
            m_ref[n, at, :] = y[:NODES] + y[NODES:] + dot_nn(four_hi, x_lo)
            return carry

        lax.fori_loop(0, BLOCK // 128, columns, 0)

    wait_arrivals(p_arrival)
    wait_arrivals(part_arrival)
    inside = [jnp.where(has_prev, 1.0, 0.0).astype(F32), None, jnp.where(has_next, 1.0, 0.0).astype(F32)]
    totals = [part[b, 0] + part[b, 1] + (part[b, 2] + part[b, 3]) for b in range(3)]

    lane2 = lax.broadcasted_iota(jnp.int32, (KC, PLANE), 1)
    row2 = lax.broadcasted_iota(jnp.int32, (KC, PLANE), 0)

    def field(layer, r):
        b, l = divmod(layer + 4, 4)
        return jnp.broadcast_to(totals[b][r : r + 1, l * PLANE : (l + 1) * PLANE], (KC, PLANE))

    def plane_neighbours(x):
        west = jnp.where(lane2 % SIDE == 0, 0.0, pltpu.roll(x, 1, 1))
        east = jnp.where(lane2 % SIDE == SIDE - 1, 0.0, pltpu.roll(x, PLANE - 1, 1))
        north = jnp.where(lane2 < SIDE, 0.0, pltpu.roll(x, SIDE, 1))
        south = jnp.where(lane2 >= PLANE - SIDE, 0.0, pltpu.roll(x, PLANE - SIDE, 1))
        return west + east + (north + south)

    states = [{}]
    for layer in range(-4, 8):
        b, l = divmod(layer + 4, 4)
        states[0][layer] = jnp.where(row2 == 0, jnp.broadcast_to(p0[b, l], (KC, PLANE)), 0.0)
    gases = []
    fields = {}

    def field_of(layer, r):
        if (layer, r) not in fields:
            fields[layer, r] = field(layer, r)
        return fields[layer, r]

    for s in range(4):
        gas = {}
        reach = 3 - s
        for layer in range(-reach, LAYERS + reach):
            g = jnp.where(row2 == 0, field_of(layer, s), 0.0)
            for m in range(s + 1):
                g = g + field_of(layer, 4 + m) * (0.5 * states[s - m][layer])
            gas[layer] = g
        gases.append(gas)
        new = {}
        for layer in range(-reach, LAYERS + reach):
            x = states[s][layer]
            around = plane_neighbours(x) + (states[s][layer - 1] + states[s][layer + 1])
            x = x + 0.15 * (around - 6.0 * x) + 0.1 * gas[layer] - 0.2 * x
            x = x + jnp.where(row2 == s + 1, 0.2, 0.0)
            if layer < 0:
                x = x * inside[0]
            if layer >= LAYERS:
                x = x * inside[2]
            new[layer] = x
        states.append(new)

    packed = jnp.zeros((KC, 128), F32)
    for s in range(4):
        t = gases[s][0] + gases[s][1] + (gases[s][2] + gases[s][3])
        t = jnp.sum(t[:, :128] + t[:, 128:], axis=1, keepdims=True)
        packed = packed + jnp.where(jnp.logical_and(lane == s * 4 + row, row < 4), t, 0.0)
    packed = jnp.sum(packed, axis=0, keepdims=True)
    slot_a = yy * 2 + core
    slot_b = xx * 2 + zh
    srow[0] = packed
    acc_a[slot_a] = packed

    def a_copy(d):
        return pltpu.make_async_remote_copy(
            src_ref=srow.at[0], dst_ref=acc_a.at[slot_a], send_sem=a_send.at[d],
            recv_sem=a_recv.at[slot_a], device_id=(stage_a_peer(d), cls), device_id_type=MESH)

    for d in range(1, 8):
        a_copy(d).start()
    for d in range(1, 8):
        s = (slot_a + d) % 8
        pltpu.make_async_copy(acc_a.at[s], acc_a.at[s], a_recv.at[s]).wait()
    total = acc_a[0]
    for s in range(1, 8):
        total = total + acc_a[s]
    srow[1] = total
    acc_b[slot_b] = total

    def b_copy(i, x, z, k):
        return pltpu.make_async_remote_copy(
            src_ref=srow.at[1], dst_ref=acc_b.at[slot_b], send_sem=b_send.at[i],
            recv_sem=b_recv.at[slot_b], device_id=(block_at(x, z, yy, core), k), device_id_type=MESH)

    same = [b_copy(d, (xx + d) % 4, zh, cls) for d in range(1, 4)]
    across = [
        b_copy(4 + 2 * d + e, (xx + d) % 4, 1 - zh, k) for d in range(4) for e, k in ((0, near), (1, near2))
    ]

    @pl.when(is_edge)
    def _():
        for copy in across:
            copy.start()

    for copy in same:
        copy.start()
    for d in range(1, 8):
        s = (slot_b + d) % 8
        pltpu.make_async_copy(acc_b.at[s], acc_b.at[s], b_recv.at[s]).wait()
    total = acc_b[0]
    for s in range(1, 8):
        total = total + acc_b[s]

    def coefficient(s, r):
        return total[:, s * 4 + r : s * 4 + r + 1]

    chambers = []
    for s in range(4):
        t = coefficient(s, 0)
        for r in range(s):
            t = t + chambers[r] * coefficient(s, r + 1)
        chambers.append(1.5 - 0.5 * (t / NCELLS))
    weights = jnp.where(row2 == 0, 1.0, 0.0)
    for r in range(3):
        weights = jnp.where(row2 == r + 1, chambers[r], weights)

    for layer in range(LAYERS):
        at = pl.ds(layer * PLANE, PLANE)
        for s in range(4):
            walls_ref[s : s + 1, at] = 0.5 * jnp.sum(weights * states[s][layer], axis=0, keepdims=True)
        pbuf[layer] = jnp.sum(weights * states[4][layer], axis=0, keepdims=True) + 0.2 * chambers[3]
    pout_ref[...] = pbuf[cls]

    wait_sends(p_copy)
    wait_sends(part_copy)
    for d in range(1, 8):
        a_copy(d).wait_send()

    @pl.when(is_edge)
    def _():
        for copy in across:
            copy.wait_send()

    for copy in same:
        copy.wait_send()


def finish_kernel(m_ref, walls_ref, vec_ref, p_ref, out_hbm, pout_ref, out_v, sem):
    pout_ref[...] = p_ref[...]
    copies = []
    for i in range(CHUNKS):
        walls = [jnp.broadcast_to(walls_ref[s : s + 1, i * 128 : (i + 1) * 128], (KC, 128)) for s in range(4)]
        for j in range(NODES):
            at = pl.ds(j * KC, KC)
            y = m_ref[i, at, :]
            for s in range(4):
                y = y + vec_ref[s, at, :] * walls[s]
            out_v[i, at, :] = y
        copies.append(pltpu.make_async_copy(out_v.at[i], out_hbm.at[:, pl.ds(i * 128, 128)], sem.at[i]))
        copies[-1].start()
    for copy in copies:
        copy.wait()


def shards(melt, counts, pressure, propagator, coupling, flux_weights):
    vmem = pl.BlockSpec(memory_space=pltpu.VMEM)
    hbm = pl.BlockSpec(memory_space=pltpu.HBM)
    dma = pltpu.SemaphoreType.DMA
    m, walls, vec, pout = pl.pallas_call(
        main_kernel,
        name="block_step",
        out_shape=(
            jax.ShapeDtypeStruct((CHUNKS, NODES * KC, 128), F32),
            jax.ShapeDtypeStruct((4, BLOCK), F32),
            jax.ShapeDtypeStruct((4, NODES * KC, 128), F32),
            jax.ShapeDtypeStruct((1, PLANE), F32),
        ),
        in_specs=[hbm] * 6,
        out_specs=(vmem, vmem, vmem, vmem),
        scratch_shapes=[
            pltpu.VMEM((CHUNKS, NODES * KC, 128), F32),
            pltpu.VMEM((KC, BLOCK), jnp.int32),
            pltpu.VMEM((KC * NODES, NODES), F32),
            pltpu.VMEM((KC, NODES), F32),
            pltpu.VMEM((KC, NODES), F32),
            pltpu.VMEM((3, 4, KC, BLOCK), F32),
            pltpu.VMEM((3, 4, 1, PLANE), F32),
            pltpu.VMEM((8, 1, 128), F32),
            pltpu.VMEM((8, 1, 128), F32),
            pltpu.VMEM((2, 1, 128), F32),
            pltpu.VMEM((LAYERS, 1, PLANE), F32),
            dma((CHUNKS,)), dma((5,)),
            dma((3, 4)), dma((3, 4)), dma((3, 4)), dma((3, 4)),
            dma((8,)), dma((8,)), dma((12,)), dma((8,)),
        ],
        compiler_params=pltpu.CompilerParams(collective_id=0, has_side_effects=True, vmem_limit_bytes=32 << 20),
    )(
        *(
            pltpu.with_memory_space_constraint(x, pltpu.HBM)
            for x in (
                melt.reshape(NODES * KC, BLOCK), counts, pressure,
                propagator.reshape(CLASSES * NODES, NODES), coupling, flux_weights,
            )
        )
    )
    shells, pout = pl.pallas_call(
        finish_kernel,
        name="walls_into_shells",
        out_shape=(
            jax.ShapeDtypeStruct((NODES * KC, BLOCK), F32),
            jax.ShapeDtypeStruct((1, PLANE), F32),
        ),
        in_specs=[vmem, vmem, vmem, vmem],
        out_specs=(hbm, vmem),
        scratch_shapes=[pltpu.VMEM((CHUNKS, NODES * KC, 128), F32), dma((CHUNKS,))],
        compiler_params=pltpu.CompilerParams(vmem_limit_bytes=32 << 20),
    )(m, walls, vec, pout)
    return shells.reshape(NODES, KC, BLOCK), pout


def solution(mesh):
    placed = (P(None, "cls", "cell"), P("cls", "cell"), P(("cell", "cls"), None), P(), P(), P())
    return jax.shard_map(
        shards,
        mesh=mesh,
        in_specs=placed,
        out_specs=(P(None, "cls", "cell"), P(("cell", "cls"), None)),
        check_vma=False,
    )
```

time: 446 us -> 35.8 us (0.08)
  blocking collectives: 372 us -> 0 us
  Pallas kernels: 0 us -> 35 us
  starting transfers between devices: 32.2 us -> 0 us
  matrix products: 21.6 us -> 0 us
  local copies, waits for them, and re-layouts: 10.6 us -> 0 us
  other arithmetic: 4.92 us -> 0 us
    psum x4 -> x0, blocking collectives: 315 us -> none  [pressure_update(): total = lax.psum(jnp.sum(gas_tile), ('cell', 'cls'))]
    pallas_call x0 -> x2, Pallas kernels: none -> 35 us  [the longest x1 33 us: shards(): pl.pallas_call(main_kernel, name='block_step', out_shape=(jax.ShapeDtypeS...]
    ppermute x8 -> x0, starting transfers between devices: 32.2 us -> none  [the longest x4 17 us: extended_2(): lax.ppermute(lax.slice_in_dim(block, 0, width, axis=dim), axis, backward)]
    unnamed x4 -> x0, blocking collectives: 30.7 us -> none
    all_gather x4 -> x0, blocking collectives: 26.3 us -> none  [shards(): block_pressure = lax.all_gather(tile.reshape(-1), 'cls', axis=0, tiled=True)]
    dot_general x8 -> x0, matrix products: 21.6 us -> none  [the longest x4 15.2 us: shell_update(): jnp.einsum('kij,jkc->ikc', propagator, shells, precision=lax.Precision.HI...]
    unnamed x16 -> x0, local copies, waits for them, and re-layouts: 8.8 us -> none
  transfers between devices with their start and end apart: 8 -> 0, of which waited for: 0 -> 0; matrix products, arithmetic and copies ran while one was open for 7% -> 0% of each run, Pallas kernels for 0% -> 0%
where the time goes in v1:
time: 35.8 us; the launch traced here: 35.7 us
  Pallas kernels  35 us (98%)
  between operations  0.64 us (2%)
    pallas_call x1, Pallas kernels, shards(): pl.pallas_call(main_kernel, name='block_step', out_shape=(jax.ShapeDtypeS...  33 us
    pallas_call x1, Pallas kernels, shards(): pl.pallas_call(finish_kernel, name='walls_into_shells', out_shape=(jax.Sh...  2.01 us

profile of v1, /device:TPU:1, one launch (start us, length us, event | category | flops | bytes accessed | tf_op | source)
XLA Modules:
  0.0 35.7 jit_solution(13367627733880419233)
XLA Ops:
  0.6 33.0 %block_step.1 = (f32[8,512,128]{2,1,0:T(8,128)S(1)}, f32[4,1024]{1,0:T(4,128)S(1)}, f32[4,512,128]{2,1,0:T(8,128)S(1)}, f32[1,256]{1,0:T(1,128)S(1)}) custom-call(f32[512,1024]{1,0:T(8,128)} %bitcast.3, s32[8,1024]{1,0:T(8,128)} %counts_hbm.1, f32[1,256]{1,0:T(1,128)} %pres_ref.1, f32[2048,64]{1,0:T(8,128)} %bitcast.4, f32[32,64]{1,0:T(8,128)} %coup_hbm.1, ...), custom_call_target="tpu_custom_call" | custom-call | tf_op jit(solution)/shard_map/block_step/pallas_call | solution.py:422
  33.7 2.0 %walls_into_shells.1 = (f32[512,1024]{1,0:T(8,128)}, f32[1,256]{1,0:T(1,128)}) custom-call(f32[8,512,128]{2,1,0:T(8,128)S(1)} %get-tuple-element.8.m_ref, f32[4,1024]{1,0:T(4,128)S(1)} %get-tuple-element.9.walls_ref, f32[4,512,128]{2,1,0:T(8,128)S(1)} %get-tuple-element.10.vec_ref, f32[1,256]{1,0:T(1,128)S(1)} %get-tuple-element.11.p_ref), custom_call_target="tpu_custom_call" | custom-call | tf_op jit(solution)/shard_map/walls_into_shells/pallas_call | solution.py:459

commit v2 on v1

--- a/solution.py
+++ b/solution.py
@@ -20,6 +20,24 @@
 NCELLS = 65536
 COUNT_SCALE = 400.0
 CHUNKS = 8
+GROUPS = 8
+
+
+class Many:
+    def __init__(self, copies):
+        self.copies = copies
+
+    def start(self):
+        for copy in self.copies:
+            copy.start()
+
+    def wait(self):
+        for copy in self.copies:
+            copy.wait()
+
+    def wait_send(self):
+        for copy in self.copies:
+            copy.wait_send()
 
 
 def split2(x):
@@ -39,8 +57,8 @@
 def main_kernel(
     melt_hbm, counts_hbm, pres_ref, prop_hbm, coup_hbm, fw_hbm,
     m_ref, walls_ref, vec_ref, pout_ref,
-    melt_v, counts_ref, prop_v, coup_v, fw_v, part, p0, acc_a, acc_b, srow, pbuf,
-    load_sem, small_sem, part_send, part_recv, p_send, p_recv, a_send, a_recv, b_send, b_recv,
+    melt_v, melt_hi, counts_ref, prop_v, coup_v, fw_v, part, p0, acc, srow, pbuf,
+    load_sem, small_sem, part_send, part_recv, p_send, p_recv, s_send, s_recv, ready,
 ):
     cell = lax.axis_index("cell")
     cls = lax.axis_index("cls")
@@ -91,6 +109,11 @@
     for d in range(4):
         signal(block_at((xx + d) % 4, 1 - zh, yy, core), source)
 
+    @pl.when(is_edge)
+    def _():
+        for d in range(4):
+            signal(block_at((xx + d) % 4, 1 - zh, yy, core), near2)
+
     @pl.when(has_prev)
     def _():
         for k in range(4):
@@ -100,23 +123,25 @@
     def _():
         for k in range(4):
             signal(cell + 1, k)
-
-    one = jnp.int32(1)
-    greeted = 13 + 8 * jnp.where(is_edge, one, 0) + 4 * jnp.where(has_prev, one, 0) + 4 * jnp.where(has_next, one, 0)
-    pl.semaphore_wait(barrier, greeted)
 
     def p_copy(rel, d, c, k):
         return pltpu.make_async_remote_copy(
             src_ref=pres_ref, dst_ref=p0.at[rel, cls], send_sem=p_send.at[rel, d],
             recv_sem=p_recv.at[rel, cls], device_id=(c, k), device_id_type=MESH)
 
-    def part_copy(rel, d, c, k):
-        lo = {0: PLANE, 1: 0, 2: 0}[rel]
-        n = {0: 3 * PLANE, 1: BLOCK, 2: 3 * PLANE}[rel]
-        return pltpu.make_async_remote_copy(
-            src_ref=part.at[1, cls, :, pl.ds(lo, n)], dst_ref=part.at[rel, cls, :, pl.ds(lo, n)],
-            send_sem=part_send.at[rel, d], recv_sem=part_recv.at[rel, cls],
-            device_id=(c, k), device_id_type=MESH)
+    def part_copies(rel, d, c, k):
+        pieces = {0: ((2, 1), (4, 2), (6, 3)), 1: ((8, None),), 2: ((6, 0), (4, 1), (2, 2))}[rel]
+        out = []
+        for i, (n, layer) in enumerate(pieces):
+            lo, size = (0, BLOCK) if layer is None else (layer * PLANE, PLANE)
+            out.append(pltpu.make_async_remote_copy(
+                src_ref=part.at[1, cls, pl.ds(0, n), pl.ds(lo, size)],
+                dst_ref=part.at[rel, cls, pl.ds(0, n), pl.ds(lo, size)],
+                send_sem=part_send.at[rel, d, i], recv_sem=part_recv.at[rel, cls, i],
+                device_id=(c, k), device_id_type=MESH))
+        return Many(out)
+
+    part_copy = part_copies
 
     def send_all(make):
         for d in range(1, 4):
@@ -150,10 +175,13 @@
         return pltpu.make_async_copy(p0.at[rel, k], p0.at[rel, k], p_recv.at[rel, k])
 
     def part_arrival(rel, k):
-        lo = {0: PLANE, 1: 0, 2: 0}[rel]
-        n = {0: 3 * PLANE, 1: BLOCK, 2: 3 * PLANE}[rel]
-        ref = part.at[rel, k, :, pl.ds(lo, n)]
-        return pltpu.make_async_copy(ref, ref, part_recv.at[rel, k])
+        pieces = {0: ((2, 1), (4, 2), (6, 3)), 1: ((8, None),), 2: ((6, 0), (4, 1), (2, 2))}[rel]
+        out = []
+        for i, (n, layer) in enumerate(pieces):
+            lo, size = (0, BLOCK) if layer is None else (layer * PLANE, PLANE)
+            ref = part.at[rel, k, pl.ds(0, n), pl.ds(lo, size)]
+            out.append(pltpu.make_async_copy(ref, ref, part_recv.at[rel, k, i]))
+        return Many(out)
 
     def wait_arrivals(arrival):
         for d in range(1, 4):
@@ -169,7 +197,6 @@
             for k in range(4):
                 arrival(2, k).wait()
 
-    send_all(p_copy)
 
     @pl.when(jnp.logical_not(has_prev))
     def _():
@@ -196,36 +223,56 @@
     def kron(x):
         return jnp.concatenate([jnp.where(row == 2 * v + half, x, 0.0) for v in range(4)], axis=1)
 
-    def row_step(r):
-        hi, lo = split2(kron(r))
-        y = dot_nn(jnp.concatenate([hi, lo], axis=0), pp)
+    def spread(r):
+        return jnp.concatenate(split2(kron(r)), axis=0)
+
+    def row_step(wide):
+        y = dot_nn(wide, pp)
         y = y[:KC] + y[KC:]
         return y + pltpu.roll(y, 64, 1)
 
     fw = fw_v[...]
     coup = coup_v[...]
     rs = [doubled(fw)]
+    wide = [spread(rs[0])]
     for t in range(4):
-        rs.append(row_step(rs[-1]))
+        rs.append(row_step(wide[-1]))
+        wide.append(spread(rs[-1]))
+    weights_f = jnp.concatenate(wide[1:], axis=0)
 
     counts_f = counts_ref[...].astype(F32)
-    for i, copy in enumerate(loads):
-        copy.wait()
-    acc = [[jnp.zeros((KC, 128), F32) for _ in range(CHUNKS)] for _ in range(4)]
-    for j in range(NODES):
-        factors = [jnp.broadcast_to(rs[t + 1][:, j : j + 1], (KC, 128)) for t in range(4)]
-        for i in range(CHUNKS):
-            node = melt_v[i, pl.ds(j * KC, KC), :]
-            for t in range(4):
-                acc[t][i] = acc[t][i] + factors[t] * node
+    flux = [[] for _ in range(4)]
+    for n in range(CHUNKS // 2):
+        loads[2 * n].wait()
+        loads[2 * n + 1].wait()
+        for k in range(KC):
+            at = pl.ds(k, NODES, stride=KC)
+            pair = jnp.concatenate([melt_v[2 * n, at, :], melt_v[2 * n + 1, at, :]], axis=1)
+            melt_hi[pl.ds(k * NODES, NODES), pl.ds(n * 256, 256)] = pair.astype(BF16)
+        y = dot_nn(weights_f, melt_hi[:, pl.ds(n * 256, 256)])
+        for t in range(4):
+            flux[t].append(y[16 * t : 16 * t + 8] + y[16 * t + 8 : 16 * t + 16])
     scale = 1.0 / (COUNT_SCALE * CLASSES)
     for t in range(4):
-        flux = jnp.concatenate(acc[t], axis=1)
-        part[1, cls, t : t + 1, :] = jnp.sum(counts_f * flux, axis=0, keepdims=True) * scale
+        flux_t = jnp.concatenate(flux[t], axis=1)
+        part[1, cls, 2 * t : 2 * t + 1, :] = jnp.sum(counts_f * flux_t, axis=0, keepdims=True) * scale
         a_t = jnp.sum(rs[t][:, :NODES] * coup, axis=1, keepdims=True)
-        part[1, cls, 4 + t : 5 + t, :] = jnp.sum(counts_f * a_t, axis=0, keepdims=True) * scale
-
+        part[1, cls, 2 * t + 1 : 2 * t + 2, :] = jnp.sum(counts_f * a_t, axis=0, keepdims=True) * scale
+
+    one = jnp.int32(1)
+    greeted = 17 + 4 * jnp.where(is_edge, one, 0) + 4 * jnp.where(has_prev, one, 0) + 4 * jnp.where(has_next, one, 0)
+    pl.semaphore_wait(barrier, greeted)
+
+    send_all(p_copy)
     send_all(part_copy)
+
+    def announce(c, k):
+        pl.semaphore_signal(ready, inc=1, device_id=(c, k), device_id_type=MESH)
+
+    for d in range(1, 4):
+        announce(block_at((xx + d) % 4, zh, yy, core), cls)
+    for d in range(4):
+        announce(block_at((xx + d) % 4, 1 - zh, yy, core), source)
 
     def col_step(v):
         hi, lo = split2(v[:, :NODES])
@@ -246,19 +293,18 @@
             vec_ref[s, pl.ds(j * KC, KC), :] = jnp.broadcast_to(vs[3 - s][:, j : j + 1], (KC, 128))
 
     for k in range(KC):
-        one = split2(prop[k * NODES : (k + 1) * NODES, :])
-        two = split2(dot3(one, one))
+        base = split2(prop[k * NODES : (k + 1) * NODES, :])
+        two = split2(dot3(base, base))
         four_hi, four_lo = split2(dot3(two, two))
-        lhs = jnp.concatenate([four_hi, four_lo], axis=0)
-
-        def columns(n, carry, lhs=lhs, four_hi=four_hi, k=k):
-            at = pl.ds(k, NODES, stride=KC)
-            x_hi, x_lo = split2(melt_v[n, at, :])
-            y = dot_nn(lhs, x_hi)
-            m_ref[n, at, :] = y[:NODES] + y[NODES:] + dot_nn(four_hi, x_lo)
-            return carry
-
-        lax.fori_loop(0, BLOCK // 128, columns, 0)
+        lhs = jnp.concatenate([four_hi, four_hi, four_lo], axis=1)
+        at = pl.ds(k, NODES, stride=KC)
+        for n in range(CHUNKS // 2):
+            x = jnp.concatenate([melt_v[2 * n, at, :], melt_v[2 * n + 1, at, :]], axis=1)
+            x_hi = melt_hi[pl.ds(k * NODES, NODES), pl.ds(n * 256, 256)]
+            x_lo = (x - x_hi.astype(F32)).astype(BF16)
+            y = dot_nn(lhs, jnp.concatenate([x_hi, x_lo, x_hi], axis=0))
+            m_ref[2 * n, at, :] = y[:, :128]
+            m_ref[2 * n + 1, at, :] = y[:, 128:]
 
     wait_arrivals(p_arrival)
     wait_arrivals(part_arrival)
@@ -295,9 +341,9 @@
         gas = {}
         reach = 3 - s
         for layer in range(-reach, LAYERS + reach):
-            g = jnp.where(row2 == 0, field_of(layer, s), 0.0)
+            g = jnp.where(row2 == 0, field_of(layer, 2 * s), 0.0)
             for m in range(s + 1):
-                g = g + field_of(layer, 4 + m) * (0.5 * states[s - m][layer])
+                g = g + field_of(layer, 2 * m + 1) * (0.5 * states[s - m][layer])
             gas[layer] = g
         gases.append(gas)
         new = {}
@@ -319,50 +365,36 @@
         t = jnp.sum(t[:, :128] + t[:, 128:], axis=1, keepdims=True)
         packed = packed + jnp.where(jnp.logical_and(lane == s * 4 + row, row < 4), t, 0.0)
     packed = jnp.sum(packed, axis=0, keepdims=True)
-    slot_a = yy * 2 + core
-    slot_b = xx * 2 + zh
+    slot = (xx * 4 + yy) * 2 + core
     srow[0] = packed
-    acc_a[slot_a] = packed
-
-    def a_copy(d):
+    acc[zh * 32 + slot] = packed
+    pl.semaphore_wait(ready, 3 + 8 * jnp.where(is_edge, one, 0))
+
+    def sum_copy(t, z, k, sem, arrived):
         return pltpu.make_async_remote_copy(
-            src_ref=srow.at[0], dst_ref=acc_a.at[slot_a], send_sem=a_send.at[d],
-            recv_sem=a_recv.at[slot_a], device_id=(stage_a_peer(d), cls), device_id_type=MESH)
-
-    for d in range(1, 8):
-        a_copy(d).start()
-    for d in range(1, 8):
-        s = (slot_a + d) % 8
-        pltpu.make_async_copy(acc_a.at[s], acc_a.at[s], a_recv.at[s]).wait()
-    total = acc_a[0]
-    for s in range(1, 8):
-        total = total + acc_a[s]
-    srow[1] = total
-    acc_b[slot_b] = total
-
-    def b_copy(i, x, z, k):
-        return pltpu.make_async_remote_copy(
-            src_ref=srow.at[1], dst_ref=acc_b.at[slot_b], send_sem=b_send.at[i],
-            recv_sem=b_recv.at[slot_b], device_id=(block_at(x, z, yy, core), k), device_id_type=MESH)
-
-    same = [b_copy(d, (xx + d) % 4, zh, cls) for d in range(1, 4)]
-    across = [
-        b_copy(4 + 2 * d + e, (xx + d) % 4, 1 - zh, k) for d in range(4) for e, k in ((0, near), (1, near2))
-    ]
+            src_ref=srow.at[0], dst_ref=acc.at[zh * 32 + slot], send_sem=sem, recv_sem=arrived,
+            device_id=((t // 8) * 16 + z * 8 + t % 8, k), device_id_type=MESH)
 
     @pl.when(is_edge)
     def _():
-        for copy in across:
-            copy.start()
-
-    for copy in same:
-        copy.start()
-    for d in range(1, 8):
-        s = (slot_b + d) % 8
-        pltpu.make_async_copy(acc_b.at[s], acc_b.at[s], b_recv.at[s]).wait()
-    total = acc_b[0]
-    for s in range(1, 8):
-        total = total + acc_b[s]
+        def across(d, carry):
+            t = (slot + d) % 32
+            sum_copy(t, 1 - zh, near, s_send.at[1], s_recv.at[1]).start()
+            sum_copy(t, 1 - zh, near2, s_send.at[2], s_recv.at[1]).start()
+            return carry
+
+        lax.fori_loop(0, 32, across, 0)
+
+    def same(d, carry):
+        sum_copy((slot + d) % 32, zh, cls, s_send.at[0], s_recv.at[0]).start()
+        return carry
+
+    lax.fori_loop(1, 32, same, 0)
+    first31 = acc.at[pl.ds(0, 31)]
+    first32 = acc.at[pl.ds(0, 32)]
+    pltpu.make_async_copy(first31, first31, s_recv.at[0]).wait()
+    pltpu.make_async_copy(first32, first32, s_recv.at[1]).wait()
+    total = jnp.sum(acc[...], axis=0)
 
     def coefficient(s, r):
         return total[:, s * 4 + r : s * 4 + r + 1]
@@ -386,30 +418,33 @@
 
     wait_sends(p_copy)
     wait_sends(part_copy)
-    for d in range(1, 8):
-        a_copy(d).wait_send()
+    pltpu.make_async_copy(first31, first31, s_send.at[0]).wait()
 
     @pl.when(is_edge)
     def _():
-        for copy in across:
-            copy.wait_send()
-
-    for copy in same:
-        copy.wait_send()
+        pltpu.make_async_copy(first32, first32, s_send.at[1]).wait()
+        pltpu.make_async_copy(first32, first32, s_send.at[2]).wait()
 
 
 def finish_kernel(m_ref, walls_ref, vec_ref, p_ref, out_hbm, pout_ref, out_v, sem):
     pout_ref[...] = p_ref[...]
+    walls = [
+        [jnp.broadcast_to(walls_ref[s : s + 1, i * 128 : (i + 1) * 128], (KC, 128)) for i in range(CHUNKS)]
+        for s in range(4)
+    ]
     copies = []
-    for i in range(CHUNKS):
-        walls = [jnp.broadcast_to(walls_ref[s : s + 1, i * 128 : (i + 1) * 128], (KC, 128)) for s in range(4)]
-        for j in range(NODES):
+    step = NODES // GROUPS
+    for g in range(GROUPS):
+        for j in range(g * step, (g + 1) * step):
             at = pl.ds(j * KC, KC)
-            y = m_ref[i, at, :]
-            for s in range(4):
-                y = y + vec_ref[s, at, :] * walls[s]
-            out_v[i, at, :] = y
-        copies.append(pltpu.make_async_copy(out_v.at[i], out_hbm.at[:, pl.ds(i * 128, 128)], sem.at[i]))
+            v = [vec_ref[s, at, :] for s in range(4)]
+            for i in range(CHUNKS):
+                y = m_ref[i, at, :]
+                for s in range(4):
+                    y = y + v[s] * walls[s][i]
+                out_v[at, pl.ds(i * 128, 128)] = y
+        rows = pl.ds(g * step * KC, step * KC)
+        copies.append(pltpu.make_async_copy(out_v.at[rows], out_hbm.at[rows], sem.at[g]))
         copies[-1].start()
     for copy in copies:
         copy.wait()
@@ -432,19 +467,19 @@
         out_specs=(vmem, vmem, vmem, vmem),
         scratch_shapes=[
             pltpu.VMEM((CHUNKS, NODES * KC, 128), F32),
+            pltpu.VMEM((KC * NODES, BLOCK), BF16),
             pltpu.VMEM((KC, BLOCK), jnp.int32),
             pltpu.VMEM((KC * NODES, NODES), F32),
             pltpu.VMEM((KC, NODES), F32),
             pltpu.VMEM((KC, NODES), F32),
             pltpu.VMEM((3, 4, KC, BLOCK), F32),
             pltpu.VMEM((3, 4, 1, PLANE), F32),
-            pltpu.VMEM((8, 1, 128), F32),
-            pltpu.VMEM((8, 1, 128), F32),
-            pltpu.VMEM((2, 1, 128), F32),
+            pltpu.VMEM((64, 1, 128), F32),
+            pltpu.VMEM((1, 1, 128), F32),
             pltpu.VMEM((LAYERS, 1, PLANE), F32),
             dma((CHUNKS,)), dma((5,)),
-            dma((3, 4)), dma((3, 4)), dma((3, 4)), dma((3, 4)),
-            dma((8,)), dma((8,)), dma((12,)), dma((8,)),
+            dma((3, 4, 3)), dma((3, 4, 3)), dma((3, 4)), dma((3, 4)),
+            dma((3,)), dma((2,)), pltpu.SemaphoreType.REGULAR,
         ],
         compiler_params=pltpu.CompilerParams(collective_id=0, has_side_effects=True, vmem_limit_bytes=32 << 20),
     )(
@@ -465,7 +500,7 @@
         ),
         in_specs=[vmem, vmem, vmem, vmem],
         out_specs=(hbm, vmem),
-        scratch_shapes=[pltpu.VMEM((CHUNKS, NODES * KC, 128), F32), dma((CHUNKS,))],
+        scratch_shapes=[pltpu.VMEM((NODES * KC, BLOCK), F32), dma((GROUPS,))],
         compiler_params=pltpu.CompilerParams(vmem_limit_bytes=32 << 20),
     )(m, walls, vec, pout)
     return shells.reshape(NODES, KC, BLOCK), pout

time: 35.8 us -> 30 us (0.84)
  Pallas kernels: 35 us -> 29.3 us
    pallas_call x1, Pallas kernels: 33 us -> 27.3 us  [shards(): pl.pallas_call(main_kernel, name='block_step', out_shape=(jax.ShapeDtypeS...]
where the time goes in v2:
time: 30 us; the launch traced here: 29.9 us
  Pallas kernels  29.3 us (98%)
  between operations  0.64 us (2%)
    pallas_call x1, Pallas kernels, shards(): pl.pallas_call(main_kernel, name='block_step', out_shape=(jax.ShapeDtypeS...  27.3 us
    pallas_call x1, Pallas kernels, shards(): pl.pallas_call(finish_kernel, name='walls_into_shells', out_shape=(jax.Sh...  2.01 us

profile of v2, /device:TPU:1, one launch (start us, length us, event | category | flops | bytes accessed | tf_op | source)
XLA Modules:
  0.0 29.9 jit_solution(15204920850991854921)
XLA Ops:
  0.6 27.3 %block_step.1 = (f32[8,512,128]{2,1,0:T(8,128)S(1)}, f32[4,1024]{1,0:T(4,128)S(1)}, f32[4,512,128]{2,1,0:T(8,128)S(1)}, f32[1,256]{1,0:T(1,128)S(1)}) custom-call(f32[512,1024]{1,0:T(8,128)} %bitcast.3, s32[8,1024]{1,0:T(8,128)} %counts_hbm.1, f32[1,256]{1,0:T(1,128)} %pres_ref.1, f32[2048,64]{1,0:T(8,128)} %bitcast.4, f32[32,64]{1,0:T(8,128)} %coup_hbm.1, ...), custom_call_target="tpu_custom_call" | custom-call | tf_op jit(solution)/shard_map/block_step/pallas_call | solution.py:457
  27.9 2.0 %walls_into_shells.1 = (f32[512,1024]{1,0:T(8,128)}, f32[1,256]{1,0:T(1,128)}) custom-call(f32[8,512,128]{2,1,0:T(8,128)S(1)} %get-tuple-element.8.m_ref, f32[4,1024]{1,0:T(4,128)S(1)} %get-tuple-element.9.walls_ref, f32[4,512,128]{2,1,0:T(8,128)S(1)} %get-tuple-element.10.vec_ref, f32[1,256]{1,0:T(1,128)S(1)} %get-tuple-element.11.p_ref), custom_call_target="tpu_custom_call" | custom-call | tf_op jit(solution)/shard_map/walls_into_shells/pallas_call | solution.py:494

commit v3 on v2

v3 whole, which is shorter than its diff:
```python
import functools

import jax
import jax.numpy as jnp
from jax import lax
from jax.experimental import pallas as pl
from jax.experimental.pallas import tpu as pltpu
from jax.sharding import PartitionSpec as P

MESH = pl.DeviceIdType.MESH
F32 = jnp.float32
BF16 = jnp.bfloat16
NODES = 64
CLASSES = 32
SIDE = 16
PLANE = 256
LAYERS = 4
BLOCK = LAYERS * PLANE
KC = 8
NCELLS = 65536
COUNT_SCALE = 400.0
CHUNKS = 8
GROUPS = 8
FIRST = 5


HALO = tuple((r, d) for d, n in ((1, 6), (2, 4), (3, 2)) for r in range(n))
HALO_ROWS = len(HALO) + 1
OWN_ROWS = 8 * LAYERS + 1


def split2(x):
    hi = x.astype(BF16)
    return hi, (x - hi.astype(F32)).astype(BF16)


def dot_nn(a, b):
    return jnp.dot(a, b, preferred_element_type=F32)


def dot3(a, b):
    (ah, al), (bh, bl) = a, b
    return dot_nn(ah, bh) + (dot_nn(al, bh) + dot_nn(ah, bl))


def main_kernel(
    melt_hbm, counts_hbm, pres_ref, prop_hbm, coup_hbm, fw_hbm,
    m_ref, walls_ref, vec_ref, pout_ref,
    melt_v, counts_ref, prop_v, coup_v, fw_v, own, halo, halo_out, acc, srow, pbuf,
    load_sem, small_sem, own_send, own_recv, halo_send, halo_recv, s_send, s_recv, ready,
):
    cell = lax.axis_index("cell")
    cls = lax.axis_index("cls")
    core = cell % 2
    yy = (cell // 2) % 4
    zh = (cell // 8) % 2
    xx = cell // 16
    has_prev = cell > 0
    has_next = cell < 63

    loads = [
        pltpu.make_async_copy(melt_hbm.at[:, pl.ds(i * 128, 128)], melt_v.at[i], load_sem.at[i])
        for i in range(CHUNKS)
    ]
    smalls = [
        pltpu.make_async_copy(prop_hbm.at[pl.ds(cls * 512, 512)], prop_v, small_sem.at[0]),
        pltpu.make_async_copy(coup_hbm.at[pl.ds(cls * 8, 8)], coup_v, small_sem.at[1]),
        pltpu.make_async_copy(fw_hbm.at[pl.ds(cls * 8, 8)], fw_v, small_sem.at[2]),
        pltpu.make_async_copy(counts_hbm, counts_ref, small_sem.at[3]),
        pltpu.make_async_copy(pres_ref, own.at[cls, OWN_ROWS - 1], small_sem.at[4]),
        pltpu.make_async_copy(pres_ref, halo_out.at[0, HALO_ROWS - 1], small_sem.at[5]),
        pltpu.make_async_copy(pres_ref, halo_out.at[1, HALO_ROWS - 1], small_sem.at[6]),
    ]
    for copy in smalls + loads:
        copy.start()

    barrier = pltpu.get_barrier_semaphore()

    def signal(c, k):
        pl.semaphore_signal(barrier, inc=1, device_id=(c, k), device_id_type=MESH)

    def block_at(x, z, y, c):
        return ((x * 2 + z) * 4 + y) * 2 + c

    adds = jnp.logical_or(cls == 0, cls == 3)
    second = jnp.where(cls == 0, 1, 2)
    near = jnp.where(cls < 2, 3, 0)
    near2 = jnp.where(cls == 3, 1, 2)
    server = jnp.where(cls < 2, 0, 3)
    one = jnp.int32(1)

    @pl.when(has_prev)
    def _():
        for k in range(4):
            signal(cell - 1, k)

    @pl.when(has_next)
    def _():
        for k in range(4):
            signal(cell + 1, k)

    for d in range(4):
        signal(block_at((xx + d) % 4, 1 - zh, yy, core), near)
    for d in range(1, 4):
        signal(cell, (cls + d) % 4)
    for d in range(1, 4):
        signal(block_at((xx + d) % 4, zh, yy, core), server)
    for d in range(1, 8):
        signal((cell // 8) * 8 + (cell + d) % 8, cls)

    @pl.when(adds)
    def _():
        for d in range(4):
            signal(block_at((xx + d) % 4, 1 - zh, yy, core), near2)
        for d in range(1, 4):
            signal(block_at((xx + d) % 4, zh, yy, core), second)

    greeted = 17 + 7 * jnp.where(adds, one, 0) + 4 * jnp.where(has_prev, one, 0) + 4 * jnp.where(has_next, one, 0)

    def own_copy(k):
        return pltpu.make_async_remote_copy(
            src_ref=own.at[cls], dst_ref=own.at[cls], send_sem=own_send.at[k], recv_sem=own_recv.at[cls],
            device_id=(cell, k), device_id_type=MESH)

    def halo_copy(side, k):
        return pltpu.make_async_remote_copy(
            src_ref=halo_out.at[side], dst_ref=halo.at[1 - side, cls], send_sem=halo_send.at[side, k],
            recv_sem=halo_recv.at[1 - side, cls], device_id=(cell + (2 * side - 1), k), device_id_type=MESH)

    def each_copy(order, act):
        for classes in order:
            for k in classes:
                @pl.when(cls != k)
                def _(k=k):
                    act(own_copy(k))

            @pl.when(has_prev)
            def _(classes=classes):
                for k in classes:
                    act(halo_copy(0, k))

            @pl.when(has_next)
            def _(classes=classes):
                for k in classes:
                    act(halo_copy(1, k))

    @pl.when(jnp.logical_not(has_prev))
    def _():
        halo[0] = jnp.zeros((4, HALO_ROWS, 1, PLANE), F32)

    @pl.when(jnp.logical_not(has_next))
    def _():
        halo[1] = jnp.zeros((4, HALO_ROWS, 1, PLANE), F32)

    for copy in smalls:
        copy.wait()
    prop = prop_v[...]
    p_hi, p_lo = split2(prop)
    pp = jnp.concatenate([p_hi, p_lo], axis=1)
    lane = lax.broadcasted_iota(jnp.int32, (KC, 128), 1)
    row = lax.broadcasted_iota(jnp.int32, (KC, 128), 0)
    half = jnp.where(lane >= 64, 1, 0)

    def doubled(x):
        return jnp.concatenate([x, x], axis=1)

    def kron(x):
        return jnp.concatenate([jnp.where(row == 2 * v + half, x, 0.0) for v in range(4)], axis=1)

    def spread(r):
        return jnp.concatenate(split2(kron(r)), axis=0)

    def row_step(wide):
        y = dot_nn(wide, pp)
        y = y[:KC] + y[KC:]
        return y + pltpu.roll(y, 64, 1)

    fw = fw_v[...]
    coup = coup_v[...]
    wide_lane = lax.broadcasted_iota(jnp.int32, (NODES, NODES * KC), 1)
    wide_row = lax.broadcasted_iota(jnp.int32, (NODES, NODES * KC), 0)
    repeat8 = jnp.where(wide_lane // KC == wide_row, 1.0, 0.0).astype(BF16)
    own_class = (wide_lane % KC == wide_row % KC)[: 2 * KC]

    def flux_rows(r):
        both = jnp.concatenate(split2(r[:, :NODES]), axis=0)
        return jnp.where(own_class, dot_nn(both, repeat8), 0.0).astype(BF16)

    rs = [doubled(fw)]
    flux_w = []
    for t in range(4):
        rs.append(row_step(spread(rs[-1])))
        flux_w.append(flux_rows(rs[-1]))
    weights_f = jnp.concatenate(flux_w, axis=0)

    counts_f = counts_ref[...].astype(F32)
    flux = [[] for _ in range(4)]
    for n in range(CHUNKS // 2):
        loads[2 * n].wait()
        loads[2 * n + 1].wait()
        pair = jnp.concatenate([melt_v[2 * n], melt_v[2 * n + 1]], axis=1)
        y = dot_nn(weights_f, pair.astype(BF16))
        for t in range(4):
            flux[t].append(y[16 * t : 16 * t + 8] + y[16 * t + 8 : 16 * t + 16])
    scale = 1.0 / (COUNT_SCALE * CLASSES)

    def put(r, value):
        for l in range(LAYERS):
            tile = value[:, l * PLANE : (l + 1) * PLANE]
            own[cls, r * LAYERS + l] = tile
            if (r, l + 1) in HALO:
                halo_out[0, HALO.index((r, l + 1))] = tile
            if (r, LAYERS - l) in HALO:
                halo_out[1, HALO.index((r, LAYERS - l))] = tile

    for t in range(4):
        a_t = jnp.sum(rs[t][:, :NODES] * coup, axis=1, keepdims=True)
        put(2 * t + 1, jnp.sum(counts_f * a_t, axis=0, keepdims=True) * scale)
    for t in range(4):
        put(2 * t, jnp.sum(counts_f * jnp.concatenate(flux[t], axis=1), axis=0, keepdims=True) * scale)

    pl.semaphore_wait(barrier, greeted)
    each_copy(((0, 3), (1, 2)), lambda copy: copy.start())

    def announce(c, k):
        pl.semaphore_signal(ready, inc=1, device_id=(c, k), device_id_type=MESH)

    for d in range(1, 4):
        announce(block_at((xx + d) % 4, zh, yy, core), server)
    for d in range(4):
        announce(block_at((xx + d) % 4, 1 - zh, yy, core), near)

    @pl.when(jnp.logical_not(adds))
    def _():
        announce(cell, server)

    def col_step(v):
        hi, lo = split2(v[:, :NODES])
        lhs = jnp.concatenate([hi, lo], axis=0)
        nt = (((1,), (1,)), ((), ()))
        y = lax.dot_general(lhs, p_hi, nt, preferred_element_type=F32)
        y = y[:KC] + y[KC:] + lax.dot_general(hi, p_lo, nt, preferred_element_type=F32)
        z = jnp.zeros((KC, 128), F32)
        for q in range(4):
            z = z + jnp.where(row == 2 * q + half, y[:, 128 * q : 128 * (q + 1)], 0.0)
        return z + pltpu.roll(z, 64, 1)

    vs = [doubled(coup)]
    for s in range(3):
        vs.append(col_step(vs[-1]))
    for s in range(4):
        for j in range(NODES):
            vec_ref[s, pl.ds(j * KC, KC), :] = jnp.broadcast_to(vs[3 - s][:, j : j + 1], (KC, 128))

    def powers_into_melt(classes):
        for k in classes:
            base = split2(prop_v[pl.ds(k * NODES, NODES), :])
            two = split2(dot3(base, base))
            four_hi, four_lo = split2(dot3(two, two))
            lhs = jnp.concatenate([four_hi, four_hi, four_lo], axis=1)
            at = pl.ds(k, NODES, stride=KC)
            for n in range(CHUNKS // 2):
                x = jnp.concatenate([melt_v[2 * n, at, :], melt_v[2 * n + 1, at, :]], axis=1)
                x_hi, x_lo = split2(x)
                y = dot_nn(lhs, jnp.concatenate([x_hi, x_lo, x_hi], axis=0))
                m_ref[2 * n, at, :] = y[:, :128]
                m_ref[2 * n + 1, at, :] = y[:, 128:]

    powers_into_melt(range(0, FIRST))

    for d in range(1, 4):
        k = (cls + d) % 4
        pltpu.make_async_copy(own.at[k], own.at[k], own_recv.at[k]).wait()
    for side, there in ((0, has_prev), (1, has_next)):
        @pl.when(there)
        def _(side=side):
            for k in range(4):
                pltpu.make_async_copy(halo.at[side, k], halo.at[side, k], halo_recv.at[side, k]).wait()

    inside = [jnp.where(has_prev, 1.0, 0.0).astype(F32), None, jnp.where(has_next, 1.0, 0.0).astype(F32)]

    lane2 = lax.broadcasted_iota(jnp.int32, (KC, PLANE), 1)
    row2 = lax.broadcasted_iota(jnp.int32, (KC, PLANE), 0)

    def field(layer, r):
        if 0 <= layer < LAYERS:
            rows = [own[k, r * LAYERS + layer] for k in range(4)]
        else:
            side, d = (0, -layer) if layer < 0 else (1, layer - LAYERS + 1)
            rows = [halo[side, k, HALO.index((r, d))] for k in range(4)]
        return jnp.broadcast_to(rows[0] + rows[1] + (rows[2] + rows[3]), (KC, PLANE))

    def start_pressure(layer):
        if 0 <= layer < LAYERS:
            return own[layer, OWN_ROWS - 1]
        return halo[0, layer + 4, HALO_ROWS - 1] if layer < 0 else halo[1, layer - LAYERS, HALO_ROWS - 1]

    def plane_neighbours(x):
        west = jnp.where(lane2 % SIDE == 0, 0.0, pltpu.roll(x, 1, 1))
        east = jnp.where(lane2 % SIDE == SIDE - 1, 0.0, pltpu.roll(x, PLANE - 1, 1))
        north = jnp.where(lane2 < SIDE, 0.0, pltpu.roll(x, SIDE, 1))
        south = jnp.where(lane2 >= PLANE - SIDE, 0.0, pltpu.roll(x, PLANE - SIDE, 1))
        return west + east + (north + south)

    states = [{}]
    for layer in range(-4, 8):
        states[0][layer] = jnp.where(row2 == 0, jnp.broadcast_to(start_pressure(layer), (KC, PLANE)), 0.0)
    gases = []
    fields = {}

    def field_of(layer, r):
        if (layer, r) not in fields:
            fields[layer, r] = field(layer, r)
        return fields[layer, r]

    for s in range(4):
        gas = {}
        reach = 3 - s
        for layer in range(-reach, LAYERS + reach):
            g = jnp.where(row2 == 0, field_of(layer, 2 * s), 0.0)
            for m in range(s + 1):
                g = g + field_of(layer, 2 * m + 1) * (0.5 * states[s - m][layer])
            gas[layer] = g
        gases.append(gas)
        new = {}
        for layer in range(-reach, LAYERS + reach):
            x = states[s][layer]
            around = plane_neighbours(x) + (states[s][layer - 1] + states[s][layer + 1])
            x = x + 0.15 * (around - 6.0 * x) + 0.1 * gas[layer] - 0.2 * x
            x = x + jnp.where(row2 == s + 1, 0.2, 0.0)
            if layer < 0:
                x = x * inside[0]
            if layer >= LAYERS:
                x = x * inside[2]
            new[layer] = x
        states.append(new)

    packed = jnp.zeros((KC, 128), F32)
    for s in range(4):
        t = gases[s][0] + gases[s][1] + (gases[s][2] + gases[s][3])
        t = jnp.sum(t[:, :128] + t[:, 128:], axis=1, keepdims=True)
        packed = packed + jnp.where(jnp.logical_and(lane == s * 4 + row, row < 4), t, 0.0)
    packed = jnp.sum(packed, axis=0, keepdims=True)
    slot = (xx * 4 + yy) * 2 + core
    srow[0] = packed
    acc[zh * 32 + slot] = packed

    hops = [0, 1, 2, 1]
    offsets = sorted(
        ((dx, dy, dc) for dx in range(4) for dy in range(4) for dc in range(2)),
        key=lambda o: -(hops[o[0]] + hops[o[1]] + 0.3 * o[2]),
    )

    def block_of(o, z):
        return block_at((xx + o[0]) % 4, z, (yy + o[1]) % 4, (core + o[2]) % 2)

    def sum_copy(c, k, sem, arrived):
        return pltpu.make_async_remote_copy(
            src_ref=srow.at[0], dst_ref=acc.at[zh * 32 + slot], send_sem=sem, recv_sem=arrived,
            device_id=(c, k), device_id_type=MESH)

    @pl.when(adds)
    def _():
        pl.semaphore_wait(ready, 15)
        for o in offsets:
            sum_copy(block_of(o, 1 - zh), near2, s_send.at[2], s_recv.at[1]).start()
            sum_copy(block_of(o, 1 - zh), near, s_send.at[1], s_recv.at[1]).start()
            if o != (0, 0, 0):
                sum_copy(block_of(o, zh), second, s_send.at[3], s_recv.at[0]).start()
                sum_copy(block_of(o, zh), cls, s_send.at[0], s_recv.at[0]).start()

    powers_into_melt(range(FIRST, KC))
    first31 = acc.at[pl.ds(0, 31)]
    first32 = acc.at[pl.ds(0, 32)]
    pltpu.make_async_copy(first31, first31, s_recv.at[0]).wait()
    pltpu.make_async_copy(first32, first32, s_recv.at[1]).wait()
    total = jnp.sum(acc[...], axis=0)

    def coefficient(s, r):
        return total[:, s * 4 + r : s * 4 + r + 1]

    chambers = []
    for s in range(4):
        t = coefficient(s, 0)
        for r in range(s):
            t = t + chambers[r] * coefficient(s, r + 1)
        chambers.append(1.5 - 0.5 * (t / NCELLS))
    weights = jnp.where(row2 == 0, 1.0, 0.0)
    for r in range(3):
        weights = jnp.where(row2 == r + 1, chambers[r], weights)

    for layer in range(LAYERS):
        at = pl.ds(layer * PLANE, PLANE)
        for s in range(4):
            walls_ref[s : s + 1, at] = 0.5 * jnp.sum(weights * states[s][layer], axis=0, keepdims=True)
        pbuf[layer] = jnp.sum(weights * states[4][layer], axis=0, keepdims=True) + 0.2 * chambers[3]
    pout_ref[...] = pbuf[cls]

    each_copy(((0, 3), (1, 2)), lambda copy: copy.wait_send())

    @pl.when(adds)
    def _():
        pltpu.make_async_copy(first31, first31, s_send.at[0]).wait()
        pltpu.make_async_copy(first32, first32, s_send.at[1]).wait()
        pltpu.make_async_copy(first32, first32, s_send.at[2]).wait()
        pltpu.make_async_copy(first31, first31, s_send.at[3]).wait()


def finish_kernel(m_ref, walls_ref, vec_ref, p_ref, out_hbm, pout_hbm, out_v, sem):
    p_out = pltpu.make_async_copy(p_ref, pout_hbm, sem.at[GROUPS])
    p_out.start()
    walls = [
        [jnp.broadcast_to(walls_ref[s : s + 1, i * 128 : (i + 1) * 128], (KC, 128)) for i in range(CHUNKS)]
        for s in range(4)
    ]
    copies = [p_out]
    step = NODES // GROUPS
    for g in range(GROUPS):
        for j in range(g * step, (g + 1) * step):
            at = pl.ds(j * KC, KC)
            v = [vec_ref[s, at, :] for s in range(4)]
            for i in range(CHUNKS):
                y = m_ref[i, at, :]
                for s in range(4):
                    y = y + v[s] * walls[s][i]
                out_v[at, pl.ds(i * 128, 128)] = y
        rows = pl.ds(g * step * KC, step * KC)
        copies.append(pltpu.make_async_copy(out_v.at[rows], out_hbm.at[rows], sem.at[g]))
        copies[-1].start()
    for copy in copies:
        copy.wait()


def shards(melt, counts, pressure, propagator, coupling, flux_weights):
    vmem = pl.BlockSpec(memory_space=pltpu.VMEM)
    hbm = pl.BlockSpec(memory_space=pltpu.HBM)
    dma = pltpu.SemaphoreType.DMA
    m, walls, vec, pout = pl.pallas_call(
        main_kernel,
        name="block_step",
        out_shape=(
            jax.ShapeDtypeStruct((CHUNKS, NODES * KC, 128), F32),
            jax.ShapeDtypeStruct((4, BLOCK), F32),
            jax.ShapeDtypeStruct((4, NODES * KC, 128), F32),
            jax.ShapeDtypeStruct((1, PLANE), F32),
        ),
        in_specs=[hbm] * 6,
        out_specs=(vmem, vmem, vmem, vmem),
        scratch_shapes=[
            pltpu.VMEM((CHUNKS, NODES * KC, 128), F32),
            pltpu.VMEM((KC, BLOCK), jnp.int32),
            pltpu.VMEM((KC * NODES, NODES), F32),
            pltpu.VMEM((KC, NODES), F32),
            pltpu.VMEM((KC, NODES), F32),
            pltpu.VMEM((4, OWN_ROWS, 1, PLANE), F32),
            pltpu.VMEM((2, 4, HALO_ROWS, 1, PLANE), F32),
            pltpu.VMEM((2, HALO_ROWS, 1, PLANE), F32),
            pltpu.VMEM((64, 1, 128), F32),
            pltpu.VMEM((1, 1, 128), F32),
            pltpu.VMEM((LAYERS, 1, PLANE), F32),
            dma((CHUNKS,)), dma((7,)),
            dma((4,)), dma((4,)), dma((2, 4)), dma((2, 4)),
            dma((4,)), dma((2,)), pltpu.SemaphoreType.REGULAR,
        ],
        compiler_params=pltpu.CompilerParams(collective_id=0, has_side_effects=True, vmem_limit_bytes=32 << 20),
    )(
        *(
            pltpu.with_memory_space_constraint(x, pltpu.HBM)
            for x in (
                melt.reshape(NODES * KC, BLOCK), counts, pressure,
                propagator.reshape(CLASSES * NODES, NODES), coupling, flux_weights,
            )
        )
    )
    shells, pout = pl.pallas_call(
        finish_kernel,
        name="walls_into_shells",
        out_shape=(
            jax.ShapeDtypeStruct((NODES * KC, BLOCK), F32),
            jax.ShapeDtypeStruct((1, PLANE), F32),
        ),
        in_specs=[vmem, vmem, vmem, vmem],
        out_specs=(hbm, hbm),
        scratch_shapes=[pltpu.VMEM((NODES * KC, BLOCK), F32), dma((GROUPS + 1,))],
        compiler_params=pltpu.CompilerParams(vmem_limit_bytes=32 << 20),
    )(m, walls, vec, pout)
    return shells.reshape(NODES, KC, BLOCK), pout


def solution(mesh):
    placed = (P(None, "cls", "cell"), P("cls", "cell"), P(("cell", "cls"), None), P(), P(), P())
    return jax.shard_map(
        shards,
        mesh=mesh,
        in_specs=placed,
        out_specs=(P(None, "cls", "cell"), P(("cell", "cls"), None)),
        check_vma=False,
    )
```

time: 30 us -> 27.3 us (0.910)
  Pallas kernels: 29.3 us -> 26.5 us
    pallas_call x1, Pallas kernels: 27.3 us -> 25.1 us  [shards(): pl.pallas_call(main_kernel, name='block_step', out_shape=(jax.ShapeDtypeS...]
    pallas_call x1, Pallas kernels: 2.01 us -> 1.46 us  [shards(): pl.pallas_call(finish_kernel, name='walls_into_shells', out_shape=(jax.Sh...]
where the time goes in v3:
time: 27.3 us; the launch traced here: 27.2 us
  Pallas kernels  26.5 us (97%)
  between operations  0.64 us (2%)
    pallas_call x1, Pallas kernels, shards(): pl.pallas_call(main_kernel, name='block_step', out_shape=(jax.ShapeDtypeS...  25.1 us
    pallas_call x1, Pallas kernels, shards(): pl.pallas_call(finish_kernel, name='walls_into_shells', out_shape=(jax.Sh...  1.46 us

profile of v3, /device:TPU:1, one launch (start us, length us, event | category | flops | bytes accessed | tf_op | source)
XLA Modules:
  0.0 27.2 jit_solution(890737275736539912)
XLA Ops:
  0.6 25.1 %block_step.1 = (f32[8,512,128]{2,1,0:T(8,128)S(1)}, f32[4,1024]{1,0:T(4,128)S(1)}, f32[4,512,128]{2,1,0:T(8,128)S(1)}, f32[1,256]{1,0:T(1,128)S(1)}) custom-call(f32[512,1024]{1,0:T(8,128)} %bitcast.3, s32[8,1024]{1,0:T(8,128)} %counts_hbm.1, f32[1,256]{1,0:T(1,128)} %pres_ref.1, f32[2048,64]{1,0:T(8,128)} %bitcast.4, f32[32,64]{1,0:T(8,128)} %coup_hbm.1, ...), custom_call_target="tpu_custom_call" | custom-call | tf_op jit(solution)/shard_map/block_step/pallas_call | solution.py:438
  25.7 1.5 %walls_into_shells.1 = (f32[512,1024]{1,0:T(8,128)}, f32[1,256]{1,0:T(1,128)}) custom-call(f32[8,512,128]{2,1,0:T(8,128)S(1)} %get-tuple-element.8.m_ref, f32[4,1024]{1,0:T(4,128)S(1)} %get-tuple-element.9.walls_ref, f32[4,512,128]{2,1,0:T(8,128)S(1)} %get-tuple-element.10.vec_ref, f32[1,256]{1,0:T(1,128)S(1)} %get-tuple-element.11.p_ref), custom_call_target="tpu_custom_call" | custom-call | tf_op jit(solution)/shard_map/walls_into_shells/pallas_call | solution.py:475

commit v4 on v3

--- a/solution.py
+++ b/solution.py
@@ -21,7 +21,7 @@
 COUNT_SCALE = 400.0
 CHUNKS = 8
 GROUPS = 8
-FIRST = 5
+FIRST = 7
 
 
 HALO = tuple((r, d) for d, n in ((1, 6), (2, 4), (3, 2)) for r in range(n))
@@ -51,10 +51,10 @@
 ):
     cell = lax.axis_index("cell")
     cls = lax.axis_index("cls")
-    core = cell % 2
-    yy = (cell // 2) % 4
-    zh = (cell // 8) % 2
-    xx = cell // 16
+    core = lax.rem(cell, 2)
+    yy = lax.rem(lax.div(cell, 2), 4)
+    zh = lax.rem(lax.div(cell, 8), 2)
+    xx = lax.div(cell, 16)
     has_prev = cell > 0
     has_next = cell < 63
 
@@ -100,20 +100,20 @@
             signal(cell + 1, k)
 
     for d in range(4):
-        signal(block_at((xx + d) % 4, 1 - zh, yy, core), near)
+        signal(block_at(lax.rem(xx + d, 4), 1 - zh, yy, core), near)
     for d in range(1, 4):
-        signal(cell, (cls + d) % 4)
+        signal(cell, lax.rem(cls + d, 4))
     for d in range(1, 4):
-        signal(block_at((xx + d) % 4, zh, yy, core), server)
+        signal(block_at(lax.rem(xx + d, 4), zh, yy, core), server)
     for d in range(1, 8):
-        signal((cell // 8) * 8 + (cell + d) % 8, cls)
+        signal(lax.div(cell, 8) * 8 + lax.rem(cell + d, 8), cls)
 
     @pl.when(adds)
     def _():
         for d in range(4):
-            signal(block_at((xx + d) % 4, 1 - zh, yy, core), near2)
+            signal(block_at(lax.rem(xx + d, 4), 1 - zh, yy, core), near2)
         for d in range(1, 4):
-            signal(block_at((xx + d) % 4, zh, yy, core), second)
+            signal(block_at(lax.rem(xx + d, 4), zh, yy, core), second)
 
     greeted = 17 + 7 * jnp.where(adds, one, 0) + 4 * jnp.where(has_prev, one, 0) + 4 * jnp.where(has_next, one, 0)
 
@@ -129,20 +129,20 @@
 
     def each_copy(order, act):
         for classes in order:
+            @pl.when(has_prev)
+            def _(classes=classes):
+                for k in classes:
+                    act(halo_copy(0, k))
+
+            @pl.when(has_next)
+            def _(classes=classes):
+                for k in classes:
+                    act(halo_copy(1, k))
+
             for k in classes:
                 @pl.when(cls != k)
                 def _(k=k):
                     act(own_copy(k))
-
-            @pl.when(has_prev)
-            def _(classes=classes):
-                for k in classes:
-                    act(halo_copy(0, k))
-
-            @pl.when(has_next)
-            def _(classes=classes):
-                for k in classes:
-                    act(halo_copy(1, k))
 
     @pl.when(jnp.logical_not(has_prev))
     def _():
@@ -220,15 +220,15 @@
         put(2 * t, jnp.sum(counts_f * jnp.concatenate(flux[t], axis=1), axis=0, keepdims=True) * scale)
 
     pl.semaphore_wait(barrier, greeted)
-    each_copy(((0, 3), (1, 2)), lambda copy: copy.start())
+    each_copy(((0, 3),), lambda copy: copy.start())
 
     def announce(c, k):
         pl.semaphore_signal(ready, inc=1, device_id=(c, k), device_id_type=MESH)
 
     for d in range(1, 4):
-        announce(block_at((xx + d) % 4, zh, yy, core), server)
+        announce(block_at(lax.rem(xx + d, 4), zh, yy, core), server)
     for d in range(4):
-        announce(block_at((xx + d) % 4, 1 - zh, yy, core), near)
+        announce(block_at(lax.rem(xx + d, 4), 1 - zh, yy, core), near)
 
     @pl.when(jnp.logical_not(adds))
     def _():
@@ -266,10 +266,12 @@
                 m_ref[2 * n, at, :] = y[:, :128]
                 m_ref[2 * n + 1, at, :] = y[:, 128:]
 
-    powers_into_melt(range(0, FIRST))
+    powers_into_melt(range(0, 3))
+    each_copy(((1, 2),), lambda copy: copy.start())
+    powers_into_melt(range(3, FIRST))
 
     for d in range(1, 4):
-        k = (cls + d) % 4
+        k = lax.rem(cls + d, 4)
         pltpu.make_async_copy(own.at[k], own.at[k], own_recv.at[k]).wait()
     for side, there in ((0, has_prev), (1, has_next)):
         @pl.when(there)
@@ -352,7 +354,7 @@
     )
 
     def block_of(o, z):
-        return block_at((xx + o[0]) % 4, z, (yy + o[1]) % 4, (core + o[2]) % 2)
+        return block_at(lax.rem(xx + o[0], 4), z, lax.rem(yy + o[1], 4), lax.rem(core + o[2], 2))
 
     def sum_copy(c, k, sem, arrived):
         return pltpu.make_async_remote_copy(

time: 27.3 us -> 26.3 us (0.963)
  Pallas kernels: 26.5 us -> 25.5 us
    pallas_call x1, Pallas kernels: 25.1 us -> 24.1 us  [shards(): pl.pallas_call(main_kernel, name='block_step', out_shape=(jax.ShapeDtypeS...]
where the time goes in v4:
time: 26.3 us; the launch traced here: 26.2 us
  Pallas kernels  25.5 us (97%)
  between operations  0.64 us (2%)
    pallas_call x1, Pallas kernels, shards(): pl.pallas_call(main_kernel, name='block_step', out_shape=(jax.ShapeDtypeS...  24.1 us
    pallas_call x1, Pallas kernels, shards(): pl.pallas_call(finish_kernel, name='walls_into_shells', out_shape=(jax.Sh...  1.46 us

profile of v4, /device:TPU:1, one launch (start us, length us, event | category | flops | bytes accessed | tf_op | source)
XLA Modules:
  0.0 26.2 jit_solution(2687096181486913909)
XLA Ops:
  0.6 24.1 %block_step.1 = (f32[8,512,128]{2,1,0:T(8,128)S(1)}, f32[4,1024]{1,0:T(4,128)S(1)}, f32[4,512,128]{2,1,0:T(8,128)S(1)}, f32[1,256]{1,0:T(1,128)S(1)}) custom-call(f32[512,1024]{1,0:T(8,128)} %bitcast.3, s32[8,1024]{1,0:T(8,128)} %counts_hbm.1, f32[1,256]{1,0:T(1,128)} %pres_ref.1, f32[2048,64]{1,0:T(8,128)} %bitcast.4, f32[32,64]{1,0:T(8,128)} %coup_hbm.1, ...), custom_call_target="tpu_custom_call" | custom-call | tf_op jit(solution)/shard_map/block_step/pallas_call | solution.py:440
  24.7 1.5 %walls_into_shells.1 = (f32[512,1024]{1,0:T(8,128)}, f32[1,256]{1,0:T(1,128)}) custom-call(f32[8,512,128]{2,1,0:T(8,128)S(1)} %get-tuple-element.8.m_ref, f32[4,1024]{1,0:T(4,128)S(1)} %get-tuple-element.9.walls_ref, f32[4,512,128]{2,1,0:T(8,128)S(1)} %get-tuple-element.10.vec_ref, f32[1,256]{1,0:T(1,128)S(1)} %get-tuple-element.11.p_ref), custom_call_target="tpu_custom_call" | custom-call | tf_op jit(solution)/shard_map/walls_into_shells/pallas_call | solution.py:477

commit v5 on v4

--- a/solution.py
+++ b/solution.py
@@ -21,11 +21,13 @@
 COUNT_SCALE = 400.0
 CHUNKS = 8
 GROUPS = 8
-FIRST = 7
-
-
-HALO = tuple((r, d) for d, n in ((1, 6), (2, 4), (3, 2)) for r in range(n))
+FIRST = 4
+
+
+HALO = ((0, 1), (1, 1), (2, 1), (3, 1), (5, 1), (0, 2), (1, 2), (3, 2), (1, 3))
+REST = ((4, 1), (2, 2), (0, 3))
 HALO_ROWS = len(HALO) + 1
+REST_ROWS = len(REST)
 OWN_ROWS = 8 * LAYERS + 1
 
 
@@ -46,8 +48,8 @@
 def main_kernel(
     melt_hbm, counts_hbm, pres_ref, prop_hbm, coup_hbm, fw_hbm,
     m_ref, walls_ref, vec_ref, pout_ref,
-    melt_v, counts_ref, prop_v, coup_v, fw_v, own, halo, halo_out, acc, srow, pbuf,
-    load_sem, small_sem, own_send, own_recv, halo_send, halo_recv, s_send, s_recv, ready,
+    melt_v, counts_ref, prop_v, coup_v, fw_v, own, halo, halo_out, rest, rest_out, acc, srow, pbuf,
+    load_sem, small_sem, own_send, own_recv, halo_send, halo_recv, rest_send, rest_recv, s_send, s_recv, ready,
 ):
     cell = lax.axis_index("cell")
     cls = lax.axis_index("cls")
@@ -127,6 +129,22 @@
             src_ref=halo_out.at[side], dst_ref=halo.at[1 - side, cls], send_sem=halo_send.at[side, k],
             recv_sem=halo_recv.at[1 - side, cls], device_id=(cell + (2 * side - 1), k), device_id_type=MESH)
 
+    def rest_copy(side):
+        return pltpu.make_async_remote_copy(
+            src_ref=rest_out.at[side], dst_ref=rest.at[1 - side, cls], send_sem=rest_send.at[side],
+            recv_sem=rest_recv.at[1 - side, cls], device_id=(cell + (2 * side - 1), 3 - 3 * side), device_id_type=MESH)
+
+    def each_rest(act):
+        @pl.when(has_prev)
+        def _():
+            act(rest_copy(0))
+
+        @pl.when(has_next)
+        def _():
+            act(rest_copy(1))
+
+    takes_rest = (jnp.logical_and(has_prev, cls == 0), jnp.logical_and(has_next, cls == 3))
+
     def each_copy(order, act):
         for classes in order:
             @pl.when(has_prev)
@@ -144,13 +162,20 @@
                 def _(k=k):
                     act(own_copy(k))
 
-    @pl.when(jnp.logical_not(has_prev))
-    def _():
-        halo[0] = jnp.zeros((4, HALO_ROWS, 1, PLANE), F32)
-
-    @pl.when(jnp.logical_not(has_next))
-    def _():
-        halo[1] = jnp.zeros((4, HALO_ROWS, 1, PLANE), F32)
+    for side in range(2):
+        @pl.when(jnp.logical_not(takes_rest[side]))
+        def _(side=side):
+            rest[side] = jnp.zeros((4, REST_ROWS, 1, PLANE), F32)
+
+    halo[2] = jnp.zeros((4, HALO_ROWS, 1, PLANE), F32)
+    in_group = lax.rem(cell, 8)
+    waits_across = zh == 1
+    there = (has_prev, has_next)
+    crosses = (jnp.logical_and(has_prev, in_group == 0), jnp.logical_and(has_next, in_group == 7))
+    later = tuple(jnp.logical_and(c, waits_across) for c in crosses)
+    soon = tuple(jnp.logical_and(t, jnp.logical_not(l)) for t, l in zip(there, later))
+    adds_across = jnp.logical_and(jnp.logical_or(crosses[0], crosses[1]), jnp.logical_not(waits_across))
+    across_slot = jnp.where(adds_across, jnp.where(crosses[1], 1, 0), 2)
 
     for copy in smalls:
         copy.wait()
@@ -212,6 +237,10 @@
                 halo_out[0, HALO.index((r, l + 1))] = tile
             if (r, LAYERS - l) in HALO:
                 halo_out[1, HALO.index((r, LAYERS - l))] = tile
+            if (r, l + 1) in REST:
+                rest_out[0, REST.index((r, l + 1))] = tile
+            if (r, LAYERS - l) in REST:
+                rest_out[1, REST.index((r, LAYERS - l))] = tile
 
     for t in range(4):
         a_t = jnp.sum(rs[t][:, :NODES] * coup, axis=1, keepdims=True)
@@ -268,34 +297,23 @@
 
     powers_into_melt(range(0, 3))
     each_copy(((1, 2),), lambda copy: copy.start())
+    each_rest(lambda copy: copy.start())
     powers_into_melt(range(3, FIRST))
 
     for d in range(1, 4):
         k = lax.rem(cls + d, 4)
         pltpu.make_async_copy(own.at[k], own.at[k], own_recv.at[k]).wait()
-    for side, there in ((0, has_prev), (1, has_next)):
-        @pl.when(there)
-        def _(side=side):
-            for k in range(4):
-                pltpu.make_async_copy(halo.at[side, k], halo.at[side, k], halo_recv.at[side, k]).wait()
-
-    inside = [jnp.where(has_prev, 1.0, 0.0).astype(F32), None, jnp.where(has_next, 1.0, 0.0).astype(F32)]
+    def wait_halo(sides):
+        for side in range(2):
+            @pl.when(sides[side])
+            def _(side=side):
+                for k in range(4):
+                    pltpu.make_async_copy(halo.at[side, k], halo.at[side, k], halo_recv.at[side, k]).wait()
+
+    wait_halo(soon)
 
     lane2 = lax.broadcasted_iota(jnp.int32, (KC, PLANE), 1)
     row2 = lax.broadcasted_iota(jnp.int32, (KC, PLANE), 0)
-
-    def field(layer, r):
-        if 0 <= layer < LAYERS:
-            rows = [own[k, r * LAYERS + layer] for k in range(4)]
-        else:
-            side, d = (0, -layer) if layer < 0 else (1, layer - LAYERS + 1)
-            rows = [halo[side, k, HALO.index((r, d))] for k in range(4)]
-        return jnp.broadcast_to(rows[0] + rows[1] + (rows[2] + rows[3]), (KC, PLANE))
-
-    def start_pressure(layer):
-        if 0 <= layer < LAYERS:
-            return own[layer, OWN_ROWS - 1]
-        return halo[0, layer + 4, HALO_ROWS - 1] if layer < 0 else halo[1, layer - LAYERS, HALO_ROWS - 1]
 
     def plane_neighbours(x):
         west = jnp.where(lane2 % SIDE == 0, 0.0, pltpu.roll(x, 1, 1))
@@ -304,42 +322,107 @@
         south = jnp.where(lane2 >= PLANE - SIDE, 0.0, pltpu.roll(x, PLANE - SIDE, 1))
         return west + east + (north + south)
 
-    states = [{}]
-    for layer in range(-4, 8):
-        states[0][layer] = jnp.where(row2 == 0, jnp.broadcast_to(start_pressure(layer), (KC, PLANE)), 0.0)
-    gases = []
-    fields = {}
-
-    def field_of(layer, r):
-        if (layer, r) not in fields:
-            fields[layer, r] = field(layer, r)
-        return fields[layer, r]
-
-    for s in range(4):
-        gas = {}
-        reach = 3 - s
-        for layer in range(-reach, LAYERS + reach):
-            g = jnp.where(row2 == 0, field_of(layer, 2 * s), 0.0)
-            for m in range(s + 1):
-                g = g + field_of(layer, 2 * m + 1) * (0.5 * states[s - m][layer])
-            gas[layer] = g
-        gases.append(gas)
-        new = {}
-        for layer in range(-reach, LAYERS + reach):
-            x = states[s][layer]
-            around = plane_neighbours(x) + (states[s][layer - 1] + states[s][layer + 1])
-            x = x + 0.15 * (around - 6.0 * x) + 0.1 * gas[layer] - 0.2 * x
-            x = x + jnp.where(row2 == s + 1, 0.2, 0.0)
-            if layer < 0:
-                x = x * inside[0]
-            if layer >= LAYERS:
-                x = x * inside[2]
-            new[layer] = x
-        states.append(new)
+    def halo_field(slot, r, d):
+        rows = [halo[slot, k, HALO.index((r, d))] for k in range(4)]
+        return jnp.broadcast_to(rows[0] + rows[1] + (rows[2] + rows[3]), (KC, PLANE))
+
+    class Recurrence:
+        def __init__(self, sides):
+            self.slots = [jnp.where(sides[side], side, 2) for side in range(2)]
+            self.inside = [jnp.where(sides[side], 1.0, 0.0).astype(F32) for side in range(2)]
+            self.fields = {}
+            self.gases = [{} for _ in range(4)]
+            self.states = [{} for _ in range(5)]
+            for layer in range(-4, 8):
+                p = jnp.broadcast_to(self.start_pressure(layer), (KC, PLANE))
+                self.states[0][layer] = jnp.where(row2 == 0, p, 0.0)
+
+        def start_pressure(self, layer):
+            if 0 <= layer < LAYERS:
+                return own[layer, OWN_ROWS - 1]
+            side, k = (0, layer + 4) if layer < 0 else (1, layer - LAYERS)
+            return halo[self.slots[side], k, HALO_ROWS - 1]
+
+        def field(self, layer, r):
+            if (layer, r) not in self.fields:
+                if 0 <= layer < LAYERS:
+                    rows = [own[k, r * LAYERS + layer] for k in range(4)]
+                    value = jnp.broadcast_to(rows[0] + rows[1] + (rows[2] + rows[3]), (KC, PLANE))
+                else:
+                    side, d = (0, -layer) if layer < 0 else (1, layer - LAYERS + 1)
+                    if (r, d) in HALO:
+                        value = halo_field(self.slots[side], r, d)
+                    else:
+                        rows = [rest[side, k, REST.index((r, d))] for k in range(4)]
+                        value = jnp.broadcast_to(rows[0] + rows[1] + (rows[2] + rows[3]), (KC, PLANE))
+                self.fields[layer, r] = value
+            return self.fields[layer, r]
+
+        def add_gas(self, s, layers):
+            for layer in layers:
+                g = jnp.where(row2 == 0, self.field(layer, 2 * s), 0.0)
+                for m in range(s + 1):
+                    g = g + self.field(layer, 2 * m + 1) * (0.5 * self.states[s - m][layer])
+                self.gases[s][layer] = g
+
+        def advance(self, s, layers):
+            now = self.states[s]
+            for layer in layers:
+                x = now[layer]
+                around = plane_neighbours(x) + (now[layer - 1] + now[layer + 1])
+                x = x + 0.15 * (around - 6.0 * x) + 0.1 * self.gases[s][layer] - 0.2 * x
+                x = x + jnp.where(row2 == s + 1, 0.2, 0.0)
+                if layer < 0:
+                    x = x * self.inside[0]
+                if layer >= LAYERS:
+                    x = x * self.inside[1]
+                self.states[s + 1][layer] = x
+
+        def main_part(self):
+            for s in range(3):
+                reach = range(s - 2, LAYERS + 2 - s)
+                self.add_gas(s, reach)
+                self.advance(s, reach)
+            self.add_gas(3, range(LAYERS))
+
+        def last_pressure(self):
+            for s in range(3):
+                ends = (s - 3, LAYERS + 2 - s)
+                self.add_gas(s, ends)
+                self.advance(s, ends)
+            self.advance(3, range(LAYERS))
+
+    quick = Recurrence(soon)
+    quick.main_part()
+    gases = quick.gases
+
+    extra = [{} for _ in range(4)]
+    shift = [{} for _ in range(4)]
+    for s in range(1, 4):
+        for d in range(1, s + 1):
+            if d == 1:
+                inner = jnp.where(crosses[1], quick.states[s - 1][LAYERS - 1], quick.states[s - 1][0])
+            else:
+                inner = shift[s - 1][d - 1]
+            y = 0.15 * inner
+            if d in shift[s - 1]:
+                x = shift[s - 1][d]
+                around = plane_neighbours(x)
+                if d + 1 in shift[s - 1]:
+                    around = around + shift[s - 1][d + 1]
+                y = y + (x + 0.15 * (around - 6.0 * x) + 0.1 * extra[s - 1][d] - 0.2 * x)
+            shift[s][d] = y
+            g = jnp.zeros((KC, PLANE), F32)
+            for m in range(s):
+                if d in shift[s - m]:
+                    g = g + halo_field(across_slot, 2 * m + 1, d) * (0.5 * shift[s - m][d])
+            extra[s][d] = g
 
     packed = jnp.zeros((KC, 128), F32)
     for s in range(4):
         t = gases[s][0] + gases[s][1] + (gases[s][2] + gases[s][3])
+        for d in extra[s]:
+            t = t + extra[s][d]
         t = jnp.sum(t[:, :128] + t[:, 128:], axis=1, keepdims=True)
         packed = packed + jnp.where(jnp.logical_and(lane == s * 4 + row, row < 4), t, 0.0)
     packed = jnp.sum(packed, axis=0, keepdims=True)
@@ -372,6 +455,17 @@
                 sum_copy(block_of(o, zh), cls, s_send.at[0], s_recv.at[0]).start()
 
     powers_into_melt(range(FIRST, KC))
+    for side in range(2):
+        @pl.when(takes_rest[side])
+        def _(side=side):
+            for k in range(4):
+                pltpu.make_async_copy(rest.at[side, k], rest.at[side, k], rest_recv.at[side, k]).wait()
+
+    wait_halo(later)
+    exact = Recurrence(there)
+    exact.main_part()
+    exact.last_pressure()
+    states = exact.states
     first31 = acc.at[pl.ds(0, 31)]
     first32 = acc.at[pl.ds(0, 32)]
     pltpu.make_async_copy(first31, first31, s_recv.at[0]).wait()
@@ -399,6 +493,7 @@
     pout_ref[...] = pbuf[cls]
 
     each_copy(((0, 3), (1, 2)), lambda copy: copy.wait_send())
+    each_rest(lambda copy: copy.wait_send())
 
     @pl.when(adds)
     def _():
@@ -455,13 +550,15 @@
             pltpu.VMEM((KC, NODES), F32),
             pltpu.VMEM((KC, NODES), F32),
             pltpu.VMEM((4, OWN_ROWS, 1, PLANE), F32),
-            pltpu.VMEM((2, 4, HALO_ROWS, 1, PLANE), F32),
+            pltpu.VMEM((3, 4, HALO_ROWS, 1, PLANE), F32),
             pltpu.VMEM((2, HALO_ROWS, 1, PLANE), F32),
+            pltpu.VMEM((2, 4, REST_ROWS, 1, PLANE), F32),
+            pltpu.VMEM((2, REST_ROWS, 1, PLANE), F32),
             pltpu.VMEM((64, 1, 128), F32),
             pltpu.VMEM((1, 1, 128), F32),
             pltpu.VMEM((LAYERS, 1, PLANE), F32),
             dma((CHUNKS,)), dma((7,)),
-            dma((4,)), dma((4,)), dma((2, 4)), dma((2, 4)),
+            dma((4,)), dma((4,)), dma((2, 4)), dma((2, 4)), dma((2,)), dma((2, 4)),
             dma((4,)), dma((2,)), pltpu.SemaphoreType.REGULAR,
         ],
         compiler_params=pltpu.CompilerParams(collective_id=0, has_side_effects=True, vmem_limit_bytes=32 << 20),

time: 26.3 us -> 25.7 us (0.977)
  Pallas kernels: 25.5 us -> 25 us
    pallas_call x1, Pallas kernels: 24.1 us -> 23.5 us  [shards(): pl.pallas_call(main_kernel, name='block_step', out_shape=(jax.ShapeDtypeS...]
where the time goes in v5:
time: 25.7 us; the launch traced here: 25.6 us
  Pallas kernels  25 us (97%)
  between operations  0.64 us (2%)
    pallas_call x1, Pallas kernels, shards(): pl.pallas_call(main_kernel, name='block_step', out_shape=(jax.ShapeDtypeS...  23.5 us
    pallas_call x1, Pallas kernels, shards(): pl.pallas_call(finish_kernel, name='walls_into_shells', out_shape=(jax.Sh...  1.46 us

profile of v5, /device:TPU:1, one launch (start us, length us, event | category | flops | bytes accessed | tf_op | source)
XLA Modules:
  0.0 25.6 jit_solution(3235070389766834398)
XLA Ops:
  0.6 23.5 %block_step.1 = (f32[8,512,128]{2,1,0:T(8,128)S(1)}, f32[4,1024]{1,0:T(4,128)S(1)}, f32[4,512,128]{2,1,0:T(8,128)S(1)}, f32[1,256]{1,0:T(1,128)S(1)}) custom-call(f32[512,1024]{1,0:T(8,128)} %bitcast.3, s32[8,1024]{1,0:T(8,128)} %counts_hbm.1, f32[1,256]{1,0:T(1,128)} %pres_ref.1, f32[2048,64]{1,0:T(8,128)} %bitcast.4, f32[32,64]{1,0:T(8,128)} %coup_hbm.1, ...), custom_call_target="tpu_custom_call" | custom-call | tf_op jit(solution)/shard_map/block_step/pallas_call | solution.py:535
  24.2 1.5 %walls_into_shells.1 = (f32[512,1024]{1,0:T(8,128)}, f32[1,256]{1,0:T(1,128)}) custom-call(f32[8,512,128]{2,1,0:T(8,128)S(1)} %get-tuple-element.8.m_ref, f32[4,1024]{1,0:T(4,128)S(1)} %get-tuple-element.9.walls_ref, f32[4,512,128]{2,1,0:T(8,128)S(1)} %get-tuple-element.10.vec_ref, f32[1,256]{1,0:T(1,128)S(1)} %get-tuple-element.11.p_ref), custom_call_target="tpu_custom_call" | custom-call | tf_op jit(solution)/shard_map/walls_into_shells/pallas_call | solution.py:574

commit v6 on v5

--- a/solution.py
+++ b/solution.py
@@ -461,6 +461,17 @@
             for k in range(4):
                 pltpu.make_async_copy(rest.at[side, k], rest.at[side, k], rest_recv.at[side, k]).wait()
 
+    for i in range(CHUNKS):
+        l, part_of = divmod(i * 128, PLANE)
+        wall = jnp.broadcast_to(0.5 * own[l, OWN_ROWS - 1][:, part_of : part_of + 128], (KC, 128))
+
+        def first_wall(j, carry, i=i, wall=wall):
+            at = pl.ds(pl.multiple_of(j * KC, KC), KC)
+            m_ref[i, at, :] = m_ref[i, at, :] + vec_ref[0, at, :] * wall
+            return carry
+
+        lax.fori_loop(0, NODES, first_wall, 0, unroll=16)
+
     wait_halo(later)
     exact = Recurrence(there)
     exact.main_part()
@@ -487,8 +498,8 @@
 
     for layer in range(LAYERS):
         at = pl.ds(layer * PLANE, PLANE)
-        for s in range(4):
-            walls_ref[s : s + 1, at] = 0.5 * jnp.sum(weights * states[s][layer], axis=0, keepdims=True)
+        for s in range(1, 4):
+            walls_ref[s - 1 : s, at] = 0.5 * jnp.sum(weights * states[s][layer], axis=0, keepdims=True)
         pbuf[layer] = jnp.sum(weights * states[4][layer], axis=0, keepdims=True) + 0.2 * chambers[3]
     pout_ref[...] = pbuf[cls]
 
@@ -508,17 +519,17 @@
     p_out.start()
     walls = [
         [jnp.broadcast_to(walls_ref[s : s + 1, i * 128 : (i + 1) * 128], (KC, 128)) for i in range(CHUNKS)]
-        for s in range(4)
+        for s in range(3)
     ]
     copies = [p_out]
     step = NODES // GROUPS
     for g in range(GROUPS):
         for j in range(g * step, (g + 1) * step):
             at = pl.ds(j * KC, KC)
-            v = [vec_ref[s, at, :] for s in range(4)]
+            v = [vec_ref[s, at, :] for s in range(1, 4)]
             for i in range(CHUNKS):
                 y = m_ref[i, at, :]
-                for s in range(4):
+                for s in range(3):
                     y = y + v[s] * walls[s][i]
                 out_v[at, pl.ds(i * 128, 128)] = y
         rows = pl.ds(g * step * KC, step * KC)
@@ -537,7 +548,7 @@
         name="block_step",
         out_shape=(
             jax.ShapeDtypeStruct((CHUNKS, NODES * KC, 128), F32),
-            jax.ShapeDtypeStruct((4, BLOCK), F32),
+            jax.ShapeDtypeStruct((3, BLOCK), F32),
             jax.ShapeDtypeStruct((4, NODES * KC, 128), F32),
             jax.ShapeDtypeStruct((1, PLANE), F32),
         ),

time: 25.7 us -> 25.7 us (level)
  no operation moved by 1% of the time
where the time goes in v6:
time: 25.7 us; the launch traced here: 25.6 us
  Pallas kernels  24.9 us (97%)
  between operations  0.64 us (2%)
    pallas_call x1, Pallas kernels, shards(): pl.pallas_call(main_kernel, name='block_step', out_shape=(jax.ShapeDtypeS...  23.5 us
    pallas_call x1, Pallas kernels, shards(): pl.pallas_call(finish_kernel, name='walls_into_shells', out_shape=(jax.Sh...  1.44 us

profile of v6, /device:TPU:1, one launch (start us, length us, event | category | flops | bytes accessed | tf_op | source)
XLA Modules:
  0.0 25.6 jit_solution(13623009919175585800)
XLA Ops:
  0.6 23.5 %block_step.1 = (f32[8,512,128]{2,1,0:T(8,128)S(1)}, f32[3,1024]{1,0:T(4,128)S(1)}, f32[4,512,128]{2,1,0:T(8,128)S(1)}, f32[1,256]{1,0:T(1,128)S(1)}) custom-call(f32[512,1024]{1,0:T(8,128)} %bitcast.3, s32[8,1024]{1,0:T(8,128)} %counts_hbm.1, f32[1,256]{1,0:T(1,128)} %pres_ref.1, f32[2048,64]{1,0:T(8,128)} %bitcast.4, f32[32,64]{1,0:T(8,128)} %coup_hbm.1, ...), custom_call_target="tpu_custom_call" | custom-call | tf_op jit(solution)/shard_map/block_step/pallas_call | solution.py:546
  24.1 1.4 %walls_into_shells.1 = (f32[512,1024]{1,0:T(8,128)}, f32[1,256]{1,0:T(1,128)}) custom-call(f32[8,512,128]{2,1,0:T(8,128)S(1)} %get-tuple-element.8.m_ref, f32[3,1024]{1,0:T(4,128)S(1)} %get-tuple-element.9.walls_ref, f32[4,512,128]{2,1,0:T(8,128)S(1)} %get-tuple-element.10.vec_ref, f32[1,256]{1,0:T(1,128)S(1)} %get-tuple-element.11.p_ref), custom_call_target="tpu_custom_call" | custom-call | tf_op jit(solution)/shard_map/walls_into_shells/pallas_call | solution.py:585

commit v7 on v6

--- a/solution.py
+++ b/solution.py
@@ -479,6 +479,16 @@
     states = exact.states
     first31 = acc.at[pl.ds(0, 31)]
     first32 = acc.at[pl.ds(0, 32)]
+    each_copy(((0, 3), (1, 2)), lambda copy: copy.wait_send())
+    each_rest(lambda copy: copy.wait_send())
+
+    @pl.when(adds)
+    def _():
+        pltpu.make_async_copy(first31, first31, s_send.at[0]).wait()
+        pltpu.make_async_copy(first32, first32, s_send.at[1]).wait()
+        pltpu.make_async_copy(first32, first32, s_send.at[2]).wait()
+        pltpu.make_async_copy(first31, first31, s_send.at[3]).wait()
+
     pltpu.make_async_copy(first31, first31, s_recv.at[0]).wait()
     pltpu.make_async_copy(first32, first32, s_recv.at[1]).wait()
     total = jnp.sum(acc[...], axis=0)
@@ -502,16 +512,6 @@
             walls_ref[s - 1 : s, at] = 0.5 * jnp.sum(weights * states[s][layer], axis=0, keepdims=True)
         pbuf[layer] = jnp.sum(weights * states[4][layer], axis=0, keepdims=True) + 0.2 * chambers[3]
     pout_ref[...] = pbuf[cls]
-
-    each_copy(((0, 3), (1, 2)), lambda copy: copy.wait_send())
-    each_rest(lambda copy: copy.wait_send())
-
-    @pl.when(adds)
-    def _():
-        pltpu.make_async_copy(first31, first31, s_send.at[0]).wait()
-        pltpu.make_async_copy(first32, first32, s_send.at[1]).wait()
-        pltpu.make_async_copy(first32, first32, s_send.at[2]).wait()
-        pltpu.make_async_copy(first31, first31, s_send.at[3]).wait()
 
 
 def finish_kernel(m_ref, walls_ref, vec_ref, p_ref, out_hbm, pout_hbm, out_v, sem):

time: 25.7 us -> 25.7 us (level)
  no operation moved by 1% of the time
where the time goes in v7:
time: 25.7 us; the launch traced here: 25.6 us
  Pallas kernels  24.9 us (97%)
  between operations  0.64 us (2%)
    pallas_call x1, Pallas kernels, shards(): pl.pallas_call(main_kernel, name='block_step', out_shape=(jax.ShapeDtypeS...  23.5 us
    pallas_call x1, Pallas kernels, shards(): pl.pallas_call(finish_kernel, name='walls_into_shells', out_shape=(jax.Sh...  1.44 us

profile of v7, /device:TPU:1, one launch (start us, length us, event | category | flops | bytes accessed | tf_op | source)
XLA Modules:
  0.0 25.6 jit_solution(15275933337875001739)
XLA Ops:
  0.6 23.5 %block_step.1 = (f32[8,512,128]{2,1,0:T(8,128)S(1)}, f32[3,1024]{1,0:T(4,128)S(1)}, f32[4,512,128]{2,1,0:T(8,128)S(1)}, f32[1,256]{1,0:T(1,128)S(1)}) custom-call(f32[512,1024]{1,0:T(8,128)} %bitcast.3, s32[8,1024]{1,0:T(8,128)} %counts_hbm.1, f32[1,256]{1,0:T(1,128)} %pres_ref.1, f32[2048,64]{1,0:T(8,128)} %bitcast.4, f32[32,64]{1,0:T(8,128)} %coup_hbm.1, ...), custom_call_target="tpu_custom_call" | custom-call | tf_op jit(solution)/shard_map/block_step/pallas_call | solution.py:546
  24.1 1.4 %walls_into_shells.1 = (f32[512,1024]{1,0:T(8,128)}, f32[1,256]{1,0:T(1,128)}) custom-call(f32[8,512,128]{2,1,0:T(8,128)S(1)} %get-tuple-element.8.m_ref, f32[3,1024]{1,0:T(4,128)S(1)} %get-tuple-element.9.walls_ref, f32[4,512,128]{2,1,0:T(8,128)S(1)} %get-tuple-element.10.vec_ref, f32[1,256]{1,0:T(1,128)S(1)} %get-tuple-element.11.p_ref), custom_call_target="tpu_custom_call" | custom-call | tf_op jit(solution)/shard_map/walls_into_shells/pallas_call | solution.py:585
